TPU v7x, 128 devices: a whole 4x4x4 slice. The times are simulated.
128 devices in a mesh: grp: 4 (over y_lo, core), gx: 32 (over y_hi, z, x).
Axes of the slice: x: 4, y: 4 (y_hi: 2, y_lo: 2; y = y_hi * 2 + y_lo), z: 4, core: 2. Of those that a mesh axis runs over, the one named last changes fastest.
Arguments:
- ocean_fields: float32 [4, 128, 32768], P(None, 'grp', 'gx'), may hold values from -1 to 1
- tracers: float32 [19, 128, 32768], P(None, ('grp', 'gx')), may hold values from 0.1 to 4
- wet_levels: int32 [128, 512], P(('grp', 'gx')), may hold values from 0 to 64
- interaction: float32 [19, 19], replicated, may hold values from -1.25 to 1.25
Outputs:
- ocean_next: float32 [4, 128, 32768], P(None, 'grp', 'gx')
- tracers_next: float32 [19, 128, 32768], P(None, ('grp', 'gx'))
All inputs are finite; a program needn't handle non-finite values.
Results may differ from a plain program's by a relative error of at most 0.0001.
Values sent between devices are 32-bit elements; how exact they have to be, the bound alone decides.
No kernel may reach another device: no remote copies, remote signals or barrier semaphores. Data moves between devices by JAX's collectives and lax.ppermute only.
A program may use at most 128 MiB of HBM per device.

v0:
```python
import jax
import jax.numpy as jnp
from jax import lax
from jax.sharding import PartitionSpec as P

NC = 2
NB = 2


courant = 0.2
diffusion = 0.08
viscosity = 0.08
time_step = 0.1
thermal = 0.2
haline = 0.15
gravity = 0.1
coriolis = 0.5
coriolis_slope = 0.5
water_extinction = 0.04
pigment_extinction = 0.01
heating_rate = 0.5
light_half = 0.3
warming = 0.1
saturation = 0.5
reaction = 0.5


def with_halo(cells, sides, width):
    for axis, dim in sides:
        count = lax.axis_size(axis)
        ends = count - 1
        head = lax.slice_in_dim(cells, 0, width, axis=dim)
        tail = lax.slice_in_dim(cells, cells.shape[dim] - width, cells.shape[dim], axis=dim)
        cells = jnp.concatenate(
            [
                lax.ppermute(tail, axis, [(i, (i + 1) % count) for i in range(ends)]),
                cells,
                lax.ppermute(head, axis, [((i + 1) % count, i) for i in range(ends)]),
            ],
            axis=dim,
        )
    return cells


def neighbours(padded):
    centre = padded[..., 1:-1, 1:-1, :]
    cell_east = padded[..., 1:-1, 2:, :]
    cell_west = padded[..., 1:-1, :-2, :]
    cell_north = padded[..., 2:, 1:-1, :]
    cell_south = padded[..., :-2, 1:-1, :]
    return (centre, cell_east, cell_west, cell_north, cell_south)


def upper_ones(levels):
    level_ids = jnp.arange(levels)
    return (level_ids[:, None] <= level_ids[None, :]).astype(jnp.float32)


def light_profile(pigment, triangle):
    extinct = water_extinction + pigment_extinction * pigment
    optical = jnp.matmul(extinct, triangle, precision=lax.Precision.HIGHEST) - 0.5 * extinct
    return (extinct, jnp.exp(-optical))


def wet_levels_mask(depth_cells, levels):
    level_ids = jnp.arange(levels).astype(jnp.float32)
    return (level_ids < depth_cells[..., None]).astype(jnp.float32)


def upwind_change(cells, face_tuple):
    centre, cell_east, cell_west, cell_north, cell_south = cells
    face_east, face_west, face_north, face_south = face_tuple
    flux_east = jnp.maximum(face_east, 0.0) * centre + jnp.minimum(face_east, 0.0) * cell_east
    flux_west = jnp.maximum(face_west, 0.0) * cell_west + jnp.minimum(face_west, 0.0) * centre
    flux_north = jnp.maximum(face_north, 0.0) * centre + jnp.minimum(face_north, 0.0) * cell_north
    flux_south = jnp.maximum(face_south, 0.0) * cell_south + jnp.minimum(face_south, 0.0) * centre
    return courant * (flux_east - flux_west + flux_north - flux_south)


def laplacian(cells, open_faces):
    summed = open_faces[0] * (cells[1] - cells[0]) + open_faces[1] * (cells[2] - cells[0])
    return summed + open_faces[2] * (cells[3] - cells[0]) + open_faces[3] * (cells[4] - cells[0])


def ocean_update(fields_pad, depth_pad, pigment, row_index, total_rows):
    levels = fields_pad.shape[-1]
    triangle = upper_ones(levels)
    wet_pad = wet_levels_mask(depth_pad, levels)
    wet_parts = neighbours(wet_pad)
    wet_mask = wet_parts[0]
    open_faces = (
        wet_mask * wet_parts[1],
        wet_mask * wet_parts[2],
        wet_mask * wet_parts[3],
        wet_mask * wet_parts[4],
    )
    density = (haline * fields_pad[3] - thermal * fields_pad[2]) * wet_pad
    pressure = gravity * jnp.matmul(density, triangle, precision=lax.Precision.HIGHEST)
    pressure_parts = neighbours(pressure)
    zonal_parts = neighbours(fields_pad[0])
    meridional = neighbours(fields_pad[1])
    warmth = neighbours(fields_pad[2])
    salt_parts = neighbours(fields_pad[3])
    face_east = 0.5 * (zonal_parts[0] + zonal_parts[1]) * open_faces[0]
    face_west = 0.5 * (zonal_parts[0] + zonal_parts[2]) * open_faces[1]
    face_north = 0.5 * (meridional[0] + meridional[3]) * open_faces[2]
    face_south = 0.5 * (meridional[0] + meridional[4]) * open_faces[3]
    face_tuple = (face_east, face_west, face_north, face_south)
    slope_x = 0.5 * (
        open_faces[0] * (pressure_parts[1] - pressure_parts[0])
        + open_faces[1] * (pressure_parts[0] - pressure_parts[2])
    )
    slope_y = 0.5 * (
        open_faces[2] * (pressure_parts[3] - pressure_parts[0])
        + open_faces[3] * (pressure_parts[0] - pressure_parts[4])
    )
    latitude = (row_index + 0.5) / total_rows - 0.5
    coriolis_row = (coriolis + coriolis_slope * latitude)[:, None, None]
    extinct, irradiance = light_profile(pigment, triangle)
    heating = heating_rate * extinct * irradiance
    zonal_next = (
        zonal_parts[0]
        + time_step * (coriolis_row * meridional[0] - slope_x)
        + viscosity * laplacian(zonal_parts, open_faces)
    ) * wet_mask
    merid_next = (
        meridional[0]
        + time_step * (-coriolis_row * zonal_parts[0] - slope_y)
        + viscosity * laplacian(meridional, open_faces)
    ) * wet_mask
    warm_next = (
        warmth[0]
        - upwind_change(warmth, face_tuple)
        + diffusion * laplacian(warmth, open_faces)
        + heating
    ) * wet_mask
    salt_next = (
        salt_parts[0]
        - upwind_change(salt_parts, face_tuple)
        + diffusion * laplacian(salt_parts, open_faces)
    ) * wet_mask
    return (jnp.stack([zonal_next, merid_next, warm_next, salt_next]), face_tuple)


def react_tracers(advected, warmth, depth_cells, interaction):
    levels = advected.shape[-1]
    irradiance = light_profile(advected[0], upper_ones(levels))[1]
    wet_mask = wet_levels_mask(depth_cells, levels)
    growth = irradiance / (irradiance + light_half) * jnp.exp(warming * warmth) * wet_mask
    saturated = advected / (saturation + jnp.abs(advected))
    mixing = jnp.dot(
        interaction, saturated.reshape(saturated.shape[0], -1), precision=lax.Precision.HIGHEST
    )
    return advected + reaction * growth * mixing.reshape(advected.shape)


def tracer_update(padded, face_tuple, warmth, depth_cells, interaction):
    cells = neighbours(padded)
    advected = cells[0] - upwind_change(cells, face_tuple)
    return react_tracers(advected, warmth, depth_cells, interaction)


def ocean_pass(fields, depth_pad, pigment, row_index, total_rows):
    padded = with_halo(fields, (("grp", 1), ("gx", 2)), 1)
    return ocean_update(padded, depth_pad, pigment, row_index, total_rows)


def depth_margin(depth_tile):
    return with_halo(depth_tile, (("grp", 0), ("gx", 1)), 1)


def shards(ocean_fields, tracers, wet_levels, interaction):
    groups = lax.axis_size("grp")
    tile_count = lax.axis_size("gx")
    tracer_count = tracers.shape[0]
    rows_tile = ocean_fields.shape[1]
    columns_all = wet_levels.shape[1]
    levels = tracers.shape[2] // columns_all
    columns_tile = columns_all // tile_count
    total_rows = rows_tile * groups
    first_row = lax.axis_index("grp") * rows_tile
    row_index = (first_row + jnp.arange(rows_tile)).astype(jnp.float32)
    fields = ocean_fields.reshape(4, rows_tile, columns_tile, levels)
    depth_strip = wet_levels.astype(jnp.float32)
    arrived, depth_tile = (
        lax.all_to_all(tracers, "gx", split_axis=2, concat_axis=1, tiled=True),
        lax.all_to_all(depth_strip[None], "gx", split_axis=2, concat_axis=1, tiled=True),
    )
    depth_pad = depth_margin(depth_tile[0])
    depth_cells = depth_tile[0]
    stocks = arrived.reshape(tracer_count, rows_tile, columns_tile, levels)
    for coupling in range(NC):
        fields, face_tuple = ocean_pass(fields, depth_pad, stocks[0], row_index, total_rows)
        for substep in range(NB):
            padded = with_halo(stocks, (("grp", 1), ("gx", 2)), 1)
            stocks = tracer_update(padded, face_tuple, fields[2], depth_cells, interaction)
    tracers_out = lax.all_to_all(
        stocks.reshape(tracer_count, rows_tile, columns_tile * levels),
        "gx",
        split_axis=1,
        concat_axis=2,
        tiled=True,
    )
    return (fields.reshape(4, rows_tile, columns_tile * levels), tracers_out)


def solution(mesh):
    placed = (P(None, "grp", "gx"), P(None, ("grp", "gx"), None), P(("grp", "gx"), None), P())
    return jax.shard_map(
        shards,
        mesh=mesh,
        in_specs=placed,
        out_specs=(P(None, "grp", "gx"), P(None, ("grp", "gx"), None)),
        check_vma=False,
    )
```

profile of v0, /device:TPU:1, one launch (start us, length us, event | category | flops | bytes accessed | tf_op | source)
XLA Modules:
  0.0 940.1 jit_solution(1963421859823042669)
XLA Ops:
  2.2 11.3 %all-to-all-start = ((f32[1,1,512]{1,0,2:T(1,128)}), f32[1,1,512]{1,0,2:T(1,128)S(1)}, u32[]{:S(2)}, u32[]{:S(2)}) async-start(f32[1,1,512]{1,0,2:T(1,128)} %copy.150), calls=%async_computation | async-start | bytes 524288 | tf_op jit(solution)/shard_map/all_to_all | solution.py:187
  15.2 3.1 collective-permute-start
  20.3 30.5 %copy.154 = f32[19,1,32768]{0,1,2:T(1,128)} copy(f32[19,1,32768]{2,1,0:T(1,128)} %param.5) | data formatting | bytes 4980736 | tf_op args[1]
  51.4 146.5 %reduce.6 = f32[32768,19]{1,0:T(8,128)} reduce(f32[32768,1,19]{2,1,0:T(1,128)} %bitcast.113, f32[]{:T(128)} %broadcast.384), dimensions={1}, to_apply=%bitcast.101.reduce_sub_computation | reduce | bytes 4980740
  197.9 17.3 %reshape.146 = f32[32,1,19456]{2,1,0:T(1,128)} reshape(f32[32768,19]{1,0:T(8,128)} %reduce.6) | data formatting | bytes 4980736
  215.2 10.3 %all-to-all-start.1 = ((f32[32,1,19456]{2,1,0:T(1,128)}), f32[32,1,19456]{2,1,0:T(1,128)}, u32[]{:S(2)}, u32[]{:S(2)}) async-start(f32[32,1,19456]{2,1,0:T(1,128)} %reshape.146), calls=%async_computation.1 | async-start | bytes 4980736 | tf_op jit(solution)/shard_map/all_to_all | solution.py:186
  228.8 3.6 collective-permute-start.4
  232.5 10.0 %collective-permute-done.5 = f32[1,16]{1,0:T(1,128)S(1)} collective-permute-done((f32[1,16]{1,0:T(1,128)S(1)}, f32[1,16]{1,0:T(1,128)S(1)}, u32[]{:S(2)}, u32[]{:S(2)}) %collective-permute-start.5) | collective-permute-done | bytes 96 | tf_op jit(solution)/shard_map/ppermute | solution.py:38
  242.8 8.5 collective-permute-start.6
  252.6 6.2 collective-permute-done.7
  258.9 5.5 collective-permute-start.2
  266.1 3.5 collective-permute-done.3
  274.5 9.6 %reduce.7 = f32[32,19456]{1,0:T(8,128)} reduce(f32[32,1,19456]{2,1,0:T(1,128)} %all-to-all-done.1, f32[]{:T(128)} %broadcast.384), dimensions={1}, to_apply=%all_to_all.12.reduce_sub_computation | reduce | bytes 4980740 | tf_op jit(solution)/shard_map/all_to_all | solution.py:186
  284.1 29.9 %reshape.147 = f32[32768,1,19]{2,1,0:T(1,128)} reshape(f32[32,19456]{1,0:T(8,128)} %reduce.7) | data formatting | bytes 4980736
  313.9 244.8 %fusion.1 = f32[32768]{0:T(1024)S(1)} fusion(f32[19,1,32768]{0,1,2:T(1,128)} %bitcast.111), kind=kLoop, calls=%fused_computation.6 | loop fusion | flops 65536 | bytes 262144 | tf_op jit(solution)/shard_map/add | solution.py:60
  559.5 2.8 fusion.75
  562.4 6.6 collective-permute-start.8
  570.9 12.3 %copy.169 = f32[19,32,16,64]{3,1,2,0:T(8,128)} copy(f32[19,32,16,64]{0,3,2,1:T(8,128)} %bitcast.112) | data formatting | bytes 4980736 | tf_op jit(solution)/shard_map/reshape | solution.py:191
  583.3 4.0 collective-permute-start.10
  592.5 3.9 collective-permute-start.12
  600.0 5.1 collective-permute-start.15
  605.5 4.4 collective-permute-done.14
  612.5 10.9 %add_divide_fusion.3 = (f32[19,32,16,64]{3,1,2,0:T(8,128)S(1)}, f32[19,32,16,64]{3,1,2,0:T(8,128)}) fusion(f32[19,32,16,64]{3,1,2,0:T(8,128)S(1)} %copy-done.1, f32[32,16,64]{2,0,1:T(8,128)} %get-tuple-element.101, f32[19,1,16,64]{3,1,2,0:T(1,128)} %copy-done.38, f32[32,16,64]{2,0,1:T(8,128)S(1)} %copy-done.2, f32[19,1,16,64]{3,1,2,0:T(1,128)} %copy-done.36, ...), kind=kLoop, calls=%fused_computation.102 | loop fusion | flops 17432576 | bytes 9006080 | tf_op jit(solution)/shard_map/div | solution.py:150
  623.4 6.4 copy.171
  629.8 5.4 reshape.131
  635.1 2.2 fusion.83
  637.3 6.2 convolution_bitcast_fusion.3
  643.5 5.7 reshape.132
  649.2 6.3 fusion.57
  657.6 3.6 collective-permute-start.16
  664.9 5.4 collective-permute-start.19
  671.6 3.6 collective-permute-done.18
  676.9 10.9 %add_divide_fusion.2 = (f32[19,32,16,64]{3,1,2,0:T(8,128)S(1)}, f32[19,32,16,64]{3,1,2,0:T(8,128)}) fusion(f32[19,32,16,64]{3,1,2,0:T(8,128)S(1)} %fusion.57, f32[32,16,64]{2,0,1:T(8,128)} %get-tuple-element.101, f32[19,1,16,64]{3,1,2,0:T(1,128)} %copy-done.39, f32[32,16,64]{2,0,1:T(8,128)S(1)} %copy-done.3, f32[19,1,16,64]{3,1,2,0:T(1,128)} %copy-done.37, ...), kind=kLoop, calls=%fused_computation.101 | loop fusion | flops 17432576 | bytes 9006080 | tf_op jit(solution)/shard_map/div | solution.py:150
  687.8 6.4 copy.173
  694.2 5.4 reshape.133
  699.5 6.4 convolution_bitcast_fusion.2
  707.3 5.4 reshape.134
  712.8 6.3 fusion.56
  719.4 1.9 collective-permute-start.21
  721.3 3.6 collective-permute-start.20
  728.5 4.6 collective-permute-start.23
  734.5 4.1 collective-permute-done.22
  741.2 10.7 %add_divide_fusion.1 = (f32[19,32,16,64]{3,1,2,0:T(8,128)S(1)}, f32[19,32,16,64]{3,1,2,0:T(8,128)}) fusion(f32[19,32,16,64]{3,1,2,0:T(8,128)S(1)} %fusion.56, f32[32,16,64]{2,0,1:T(8,128)S(1)} %get-tuple-element.96, f32[19,1,16,64]{3,1,2,0:T(1,128)} %copy-done.40, f32[32,16,64]{2,0,1:T(8,128)S(1)} %copy-done.10, ...), kind=kLoop, calls=%fused_computation.100 | loop fusion | flops 17432576 | bytes 9006080 | tf_op jit(solution)/shard_map/div | solution.py:150
  751.9 6.4 copy.177
  758.2 4.0 reshape.135
  762.3 4.5 convolution_bitcast_fusion.1
  766.8 5.7 reshape.136
  773.9 6.3 fusion.55
  780.5 2.1 collective-permute-start.25
  782.5 3.6 collective-permute-start.24
  789.8 5.8 collective-permute-start.27
  795.6 5.1 collective-permute-done.26
  802.5 9.4 %add_divide_fusion = (f32[19,32,16,64]{3,1,2,0:T(8,128)S(1)}, f32[19,32,16,64]{3,1,2,0:T(8,128)}) fusion(f32[19,32,16,64]{3,1,2,0:T(8,128)S(1)} %fusion.55, f32[32,16,64]{2,0,1:T(8,128)S(1)} %copy-done.24, f32[19,1,16,64]{3,1,2,0:T(1,128)S(1)} %collective-permute-done.24, f32[32,16,64]{2,0,1:T(8,128)S(1)} %copy-done.10, ...), kind=kLoop, calls=%fused_computation.99 | loop fusion | flops 17432576 | bytes 9006080 | tf_op jit(solution)/shard_map/div | solution.py:150
  813.4 6.4 copy.179
  819.8 4.0 reshape.137
  823.8 4.5 convolution_bitcast_fusion
  828.3 5.4 reshape.138
  833.8 6.3 fusion.54
  840.0 5.1 copy.196
  845.2 5.4 reshape.141
  850.6 38.0 %all-to-all-start.2 = ((f32[19,32,1024]{2,0,1:T(8,128)}), f32[19,32,1024]{2,0,1:T(8,128)S(1)}, u32[]{:S(2)}, u32[]{:S(2)}) async-start(f32[19,32,1024]{2,0,1:T(8,128)} %reshape.141), calls=%async_computation.2 | async-start | bytes 6291456 | tf_op jit(solution)/shard_map/all_to_all | solution.py:197
  898.1 33.9 %all-to-all-done.2 = f32[19,32,1024]{2,0,1:T(8,128)S(1)} async-done(((f32[19,32,1024]{2,0,1:T(8,128)}), f32[19,32,1024]{2,0,1:T(8,128)S(1)}, u32[]{:S(2)}, u32[]{:S(2)}) %all-to-all-start.2) | async-done | bytes 2490400 | tf_op jit(solution)/shard_map/all_to_all | solution.py:197
  932.0 2.9 copy.183
  934.9 5.0 all_to_all.30
  (188 shorter events, 67.1 us)
Async XLA Ops:
  0.6 636.7 %copy-start = (f32[19,19]{1,0:T(8,128)S(1)}, f32[19,19]{1,0:T(8,128)}, u32[]{:S(2)}) copy-start(f32[19,19]{1,0:T(8,128)} %param.7) | copy-start | bytes 4336
  2.2 213.0 %all-to-all-start = ((f32[1,1,512]{1,0,2:T(1,128)}), f32[1,1,512]{1,0,2:T(1,128)S(1)}, u32[]{:S(2)}, u32[]{:S(2)}) async-start(f32[1,1,512]{1,0,2:T(1,128)} %copy.150), calls=%async_computation | async-start | bytes 524288 | tf_op jit(solution)/shard_map/all_to_all | solution.py:187
  15.2 243.6 %collective-permute-start = (f32[4,1,16,64]{3,1,2,0:T(1,128)S(1)}, f32[4,1,16,64]{3,1,2,0:T(1,128)S(1)}, u32[]{:S(2)}, u32[]{:S(2)}) collective-permute-start(f32[4,1,16,64]{3,1,2,0:T(1,128)S(1)} %get-tuple-element.70), channel_id=1, source_target_pairs={{0,32},{32,64},{64,96},{1,33},{33,65},{65,97},{2,34},{34,66},{66,9... | collective-permute-start | bytes 49160 | tf_op jit(solution)/shard_map/ppermute | solution.py:36
  18.4 240.4 %collective-permute-start.1 = (f32[4,1,16,64]{3,1,2,0:T(1,128)S(1)}, f32[4,1,16,64]{3,1,2,0:T(1,128)S(1)}, u32[]{:S(2)}, u32[]{:S(2)}) collective-permute-start(f32[4,1,16,64]{3,1,2,0:T(1,128)S(1)} %get-tuple-element.71), channel_id=1, source_target_pairs={{32,0},{64,32},{96,64},{33,1},{65,33},{97,65},{34,2},{66,34},{98,6... | collective-permute-start | bytes 49160 | tf_op jit(solution)/shard_map/ppermute | solution.py:38
  215.2 59.3 %all-to-all-start.1 = ((f32[32,1,19456]{2,1,0:T(1,128)}), f32[32,1,19456]{2,1,0:T(1,128)}, u32[]{:S(2)}, u32[]{:S(2)}) async-start(f32[32,1,19456]{2,1,0:T(1,128)} %reshape.146), calls=%async_computation.1 | async-start | bytes 4980736 | tf_op jit(solution)/shard_map/all_to_all | solution.py:186
  226.9 15.7 %collective-permute-start.5 = (f32[1,16]{1,0:T(1,128)S(1)}, f32[1,16]{1,0:T(1,128)S(1)}, u32[]{:S(2)}, u32[]{:S(2)}) collective-permute-start(f32[1,16]{1,0:T(1,128)S(1)} %bitcast.117), channel_id=1, source_target_pairs={{32,0},{64,32},{96,64},{33,1},{65,33},{97,65},{34,2},{66,34},{98,6... | collective-permute-start | bytes 200 | tf_op jit(solution)/shard_map/ppermute | solution.py:38
  228.8 13.8 %collective-permute-start.4 = (f32[1,16]{1,0:T(1,128)S(1)}, f32[1,16]{1,0:T(1,128)S(1)}, u32[]{:S(2)}, u32[]{:S(2)}) collective-permute-start(f32[1,16]{1,0:T(1,128)S(1)} %slice_bitcast_fusion.8), channel_id=1, source_target_pairs={{0,32},{32,64},{64,96},{1,33},{33,65},{65,97},{2,34},{34,66},{66,9... | collective-permute-start | bytes 200 | tf_op jit(solution)/shard_map/ppermute | solution.py:36
  242.8 9.8 %collective-permute-start.6 = (f32[34,1]{0,1:T(1,128)S(1)}, f32[34,1]{0,1:T(1,128)S(1)}, u32[]{:S(2)}, u32[]{:S(2)}) collective-permute-start(f32[34,1]{0,1:T(1,128)S(1)} %get-tuple-element.102), channel_id=1, source_target_pairs={{0,1},{1,2},{2,3},{3,4},{4,5},{5,6},{6,7},{7,8},{8,9},{9,10},{10,1... | collective-permute-start | bytes 416 | tf_op jit(solution)/shard_map/ppermute | solution.py:36
  251.3 7.5 collective-permute-start.7
  258.9 7.2 collective-permute-start.2
  264.4 5.2 collective-permute-start.3
  562.3 34.1 %copy-start.25 = (f32[32,16,64]{2,0,1:T(8,128)}, f32[32,16,64]{2,0,1:T(8,128)S(1)}, u32[]{:S(2)}) copy-start(f32[32,16,64]{2,0,1:T(8,128)S(1)} %fusion.75) | copy-start | bytes 393220
  562.4 20.9 %collective-permute-start.8 = (f32[4,1,16,64]{3,1,2,0:T(1,128)S(1)}, f32[4,1,16,64]{3,1,2,0:T(1,128)S(1)}, u32[]{:S(2)}, u32[]{:S(2)}) collective-permute-start(f32[4,1,16,64]{3,1,2,0:T(1,128)S(1)} %get-tuple-element.68), channel_id=1, source_target_pairs={{0,32},{32,64},{64,96},{1,33},{33,65},{65,97},{2,34},{34,66},{66,9... | collective-permute-start | bytes 49160 | tf_op jit(solution)/shard_map/ppermute | solution.py:36
  569.0 14.3 %collective-permute-start.9 = (f32[4,1,16,64]{3,1,2,0:T(1,128)S(1)}, f32[4,1,16,64]{3,1,2,0:T(1,128)S(1)}, u32[]{:S(2)}, u32[]{:S(2)}) collective-permute-start(f32[4,1,16,64]{3,1,2,0:T(1,128)S(1)} %get-tuple-element.69), channel_id=1, source_target_pairs={{32,0},{64,32},{96,64},{33,1},{65,33},{97,65},{34,2},{66,34},{98,6... | collective-permute-start | bytes 49160 | tf_op jit(solution)/shard_map/ppermute | solution.py:38
  583.3 15.3 %copy-start.1 = (f32[19,32,16,64]{3,1,2,0:T(8,128)S(1)}, f32[19,32,16,64]{3,1,2,0:T(8,128)}, u32[]{:S(2)}) copy-start(f32[19,32,16,64]{3,1,2,0:T(8,128)} %copy.169) | copy-start | bytes 7471108
  583.3 13.1 %collective-permute-start.10 = (f32[4,34,1,64]{3,1,2,0:T(8,128)S(1)}, f32[4,34,1,64]{3,1,2,0:T(8,128)S(1)}, u32[]{:S(2)}, u32[]{:S(2)}) collective-permute-start(f32[4,34,1,64]{3,1,2,0:T(8,128)S(1)} %get-tuple-element.64), channel_id=1, source_target_pairs={{0,1},{1,2},{2,3},{3,4},{4,5},{5,6},{6,7},{7,8},{8,9},{9,10},{10,1... | collective-permute-start | bytes 104456 | tf_op jit(solution)/shard_map/ppermute | solution.py:36
  587.3 9.1 collective-permute-start.11
  590.6 7.0 collective-permute-start.13
  592.5 6.1 collective-permute-start.12
  596.7 15.8 %copy-start.2 = (f32[32,16,64]{2,0,1:T(8,128)S(1)}, f32[32,16,64]{2,0,1:T(8,128)}, u32[]{:S(2)}) copy-start(f32[32,16,64]{2,0,1:T(8,128)} %get-tuple-element.86) | copy-start | bytes 393220
  596.7 15.8 %copy-start.4 = (f32[32,16,64]{2,0,1:T(8,128)S(1)}, f32[32,16,64]{2,0,1:T(8,128)}, u32[]{:S(2)}) copy-start(f32[32,16,64]{2,0,1:T(8,128)} %get-tuple-element.89) | copy-start | bytes 393220
  596.7 15.8 %copy-start.6 = (f32[32,16,64]{2,0,1:T(8,128)S(1)}, f32[32,16,64]{2,0,1:T(8,128)}, u32[]{:S(2)}) copy-start(f32[32,16,64]{2,0,1:T(8,128)} %get-tuple-element.97) | copy-start | bytes 393220
  596.7 15.8 %copy-start.8 = (f32[32,16,64]{2,0,1:T(8,128)S(1)}, f32[32,16,64]{2,0,1:T(8,128)}, u32[]{:S(2)}) copy-start(f32[32,16,64]{2,0,1:T(8,128)} %get-tuple-element.99) | copy-start | bytes 393220
  598.6 13.2 %copy-start.38 = (f32[19,1,16,64]{3,1,2,0:T(1,128)}, f32[19,1,16,64]{3,1,2,0:T(1,128)S(1)}, u32[]{:S(2)}) copy-start(f32[19,1,16,64]{3,1,2,0:T(1,128)S(1)} %collective-permute-done.12) | copy-start | bytes 233476
  598.7 11.3 %collective-permute-start.14 = (f32[19,34,1,64]{3,1,2,0:T(8,128)S(1)}, f32[19,34,1,64]{3,1,2,0:T(8,128)S(1)}, u32[]{:S(2)}, u32[]{:S(2)}) collective-permute-start(f32[19,34,1,64]{3,1,2,0:T(8,128)S(1)} %get-tuple-element.46), channel_id=1, source_target_pairs={{1,0},{2,1},{3,2},{4,3},{5,4},{6,5},{7,6},{8,7},{9,8},{10,9},{11,1... | collective-permute-start | bytes 496136 | tf_op jit(solution)/shard_map/ppermute | solution.py:38
  600.0 11.7 %collective-permute-start.15 = (f32[19,34,1,64]{3,1,2,0:T(8,128)S(1)}, f32[19,34,1,64]{3,1,2,0:T(8,128)S(1)}, u32[]{:S(2)}, u32[]{:S(2)}) collective-permute-start(f32[19,34,1,64]{3,1,2,0:T(8,128)S(1)} %get-tuple-element.47), channel_id=1, source_target_pairs={{0,1},{1,2},{2,3},{3,4},{4,5},{5,6},{6,7},{7,8},{8,9},{9,10},{10,1... | collective-permute-start | bytes 496136 | tf_op jit(solution)/shard_map/ppermute | solution.py:36
  655.7 6.9 collective-permute-start.17
  657.6 5.8 collective-permute-start.16
  662.5 14.4 %copy-start.3 = (f32[32,16,64]{2,0,1:T(8,128)S(1)}, f32[32,16,64]{2,0,1:T(8,128)}, u32[]{:S(2)}) copy-start(f32[32,16,64]{2,0,1:T(8,128)} %get-tuple-element.86) | copy-start | bytes 393220
  662.5 14.4 %copy-start.5 = (f32[32,16,64]{2,0,1:T(8,128)S(1)}, f32[32,16,64]{2,0,1:T(8,128)}, u32[]{:S(2)}) copy-start(f32[32,16,64]{2,0,1:T(8,128)} %get-tuple-element.89) | copy-start | bytes 393220
  662.5 14.4 %copy-start.7 = (f32[32,16,64]{2,0,1:T(8,128)S(1)}, f32[32,16,64]{2,0,1:T(8,128)}, u32[]{:S(2)}) copy-start(f32[32,16,64]{2,0,1:T(8,128)} %get-tuple-element.97) | copy-start | bytes 393220
  662.5 14.4 %copy-start.9 = (f32[32,16,64]{2,0,1:T(8,128)S(1)}, f32[32,16,64]{2,0,1:T(8,128)}, u32[]{:S(2)}) copy-start(f32[32,16,64]{2,0,1:T(8,128)} %get-tuple-element.99) | copy-start | bytes 393220
  662.6 9.0 copy-start.37
  663.6 11.6 %collective-permute-start.18 = (f32[19,34,1,64]{3,1,2,0:T(8,128)S(1)}, f32[19,34,1,64]{3,1,2,0:T(8,128)S(1)}, u32[]{:S(2)}, u32[]{:S(2)}) collective-permute-start(f32[19,34,1,64]{3,1,2,0:T(8,128)S(1)} %get-tuple-element.44), channel_id=1, source_target_pairs={{1,0},{2,1},{3,2},{4,3},{5,4},{6,5},{7,6},{8,7},{9,8},{10,9},{11,1... | collective-permute-start | bytes 496136 | tf_op jit(solution)/shard_map/ppermute | solution.py:38
  664.9 12.0 %collective-permute-start.19 = (f32[19,34,1,64]{3,1,2,0:T(8,128)S(1)}, f32[19,34,1,64]{3,1,2,0:T(8,128)}, u32[]{:S(2)}, u32[]{:S(2)}) collective-permute-start(f32[19,34,1,64]{3,1,2,0:T(8,128)S(1)} %get-tuple-element.45), channel_id=1, source_target_pairs={{0,1},{1,2},{2,3},{3,4},{4,5},{5,6},{6,7},{7,8},{8,9},{9,10},{10,1... | collective-permute-start | bytes 496136 | tf_op jit(solution)/shard_map/ppermute | solution.py:36
  712.8 12.2 %copy-start.27 = (f32[32,16,64]{2,0,1:T(8,128)S(1)}, f32[32,16,64]{2,0,1:T(8,128)}, u32[]{:S(2)}) copy-start(f32[32,16,64]{2,0,1:T(8,128)} %get-tuple-element.23) | copy-start | bytes 393220
  712.8 12.2 %copy-start.28 = (f32[32,16,64]{2,0,1:T(8,128)S(1)}, f32[32,16,64]{2,0,1:T(8,128)}, u32[]{:S(2)}) copy-start(f32[32,16,64]{2,0,1:T(8,128)} %get-tuple-element.82) | copy-start | bytes 393220
  712.8 12.2 %copy-start.29 = (f32[32,16,64]{2,0,1:T(8,128)S(1)}, f32[32,16,64]{2,0,1:T(8,128)}, u32[]{:S(2)}) copy-start(f32[32,16,64]{2,0,1:T(8,128)} %get-tuple-element.19) | copy-start | bytes 393220
  712.8 12.2 %copy-start.30 = (f32[32,16,64]{2,0,1:T(8,128)S(1)}, f32[32,16,64]{2,0,1:T(8,128)}, u32[]{:S(2)}) copy-start(f32[32,16,64]{2,0,1:T(8,128)} %get-tuple-element.85) | copy-start | bytes 393220
  719.4 6.8 collective-permute-start.21
  721.3 5.8 collective-permute-start.20
  726.1 15.0 %copy-start.17 = (f32[32,16,64]{2,0,1:T(8,128)}, f32[32,16,64]{2,0,1:T(8,128)S(1)}, u32[]{:S(2)}) copy-start(f32[32,16,64]{2,0,1:T(8,128)S(1)} %get-tuple-element.92) | copy-start | bytes 393220
  726.1 15.0 %copy-start.19 = (f32[32,16,64]{2,0,1:T(8,128)}, f32[32,16,64]{2,0,1:T(8,128)S(1)}, u32[]{:S(2)}) copy-start(f32[32,16,64]{2,0,1:T(8,128)S(1)} %get-tuple-element.94) | copy-start | bytes 393220
  726.1 15.0 %copy-start.21 = (f32[32,16,64]{2,0,1:T(8,128)}, f32[32,16,64]{2,0,1:T(8,128)S(1)}, u32[]{:S(2)}) copy-start(f32[32,16,64]{2,0,1:T(8,128)S(1)} %get-tuple-element.95) | copy-start | bytes 393220
  726.1 15.0 %copy-start.23 = (f32[32,16,64]{2,0,1:T(8,128)}, f32[32,16,64]{2,0,1:T(8,128)S(1)}, u32[]{:S(2)}) copy-start(f32[32,16,64]{2,0,1:T(8,128)S(1)} %get-tuple-element.96) | copy-start | bytes 393220
  726.1 15.0 %copy-start.10 = (f32[32,16,64]{2,0,1:T(8,128)S(1)}, f32[32,16,64]{2,0,1:T(8,128)}, u32[]{:S(2)}) copy-start(f32[32,16,64]{2,0,1:T(8,128)} %get-tuple-element.22) | copy-start | bytes 393220
  726.1 15.0 %copy-start.11 = (f32[32,16,64]{2,0,1:T(8,128)S(1)}, f32[32,16,64]{2,0,1:T(8,128)}, u32[]{:S(2)}) copy-start(f32[32,16,64]{2,0,1:T(8,128)} %get-tuple-element.81) | copy-start | bytes 393220
  726.1 15.0 %copy-start.13 = (f32[32,16,64]{2,0,1:T(8,128)S(1)}, f32[32,16,64]{2,0,1:T(8,128)}, u32[]{:S(2)}) copy-start(f32[32,16,64]{2,0,1:T(8,128)} %get-tuple-element.18) | copy-start | bytes 393220
  726.1 15.0 %copy-start.15 = (f32[32,16,64]{2,0,1:T(8,128)S(1)}, f32[32,16,64]{2,0,1:T(8,128)}, u32[]{:S(2)}) copy-start(f32[32,16,64]{2,0,1:T(8,128)} %get-tuple-element.84) | copy-start | bytes 393220
  727.2 11.4 %collective-permute-start.22 = (f32[19,34,1,64]{3,1,2,0:T(8,128)S(1)}, f32[19,34,1,64]{3,1,2,0:T(8,128)S(1)}, u32[]{:S(2)}, u32[]{:S(2)}) collective-permute-start(f32[19,34,1,64]{3,1,2,0:T(8,128)S(1)} %get-tuple-element.42), channel_id=1, source_target_pairs={{1,0},{2,1},{3,2},{4,3},{5,4},{6,5},{7,6},{8,7},{9,8},{10,9},{11,1... | collective-permute-start | bytes 496136 | tf_op jit(solution)/shard_map/ppermute | solution.py:38
  728.5 11.8 %collective-permute-start.23 = (f32[19,34,1,64]{3,1,2,0:T(8,128)S(1)}, f32[19,34,1,64]{3,1,2,0:T(8,128)S(1)}, u32[]{:S(2)}, u32[]{:S(2)}) collective-permute-start(f32[19,34,1,64]{3,1,2,0:T(8,128)S(1)} %get-tuple-element.43), channel_id=1, source_target_pairs={{0,1},{1,2},{2,3},{3,4},{4,5},{5,6},{6,7},{7,8},{8,9},{9,10},{10,1... | collective-permute-start | bytes 496136 | tf_op jit(solution)/shard_map/ppermute | solution.py:36
  780.2 22.3 %copy-start.12 = (f32[32,16,64]{2,0,1:T(8,128)S(1)}, f32[32,16,64]{2,0,1:T(8,128)}, u32[]{:S(2)}) copy-start(f32[32,16,64]{2,0,1:T(8,128)} %get-tuple-element.81) | copy-start | bytes 393220
  780.2 22.3 %copy-start.14 = (f32[32,16,64]{2,0,1:T(8,128)S(1)}, f32[32,16,64]{2,0,1:T(8,128)}, u32[]{:S(2)}) copy-start(f32[32,16,64]{2,0,1:T(8,128)} %get-tuple-element.18) | copy-start | bytes 393220
  780.2 22.3 %copy-start.16 = (f32[32,16,64]{2,0,1:T(8,128)S(1)}, f32[32,16,64]{2,0,1:T(8,128)}, u32[]{:S(2)}) copy-start(f32[32,16,64]{2,0,1:T(8,128)} %get-tuple-element.84) | copy-start | bytes 393220
  780.2 22.3 %copy-start.18 = (f32[32,16,64]{2,0,1:T(8,128)S(1)}, f32[32,16,64]{2,0,1:T(8,128)}, u32[]{:S(2)}) copy-start(f32[32,16,64]{2,0,1:T(8,128)} %copy-done.17) | copy-start | bytes 393220
  780.2 22.3 %copy-start.20 = (f32[32,16,64]{2,0,1:T(8,128)S(1)}, f32[32,16,64]{2,0,1:T(8,128)}, u32[]{:S(2)}) copy-start(f32[32,16,64]{2,0,1:T(8,128)} %copy-done.19) | copy-start | bytes 393220
  780.2 22.3 %copy-start.22 = (f32[32,16,64]{2,0,1:T(8,128)S(1)}, f32[32,16,64]{2,0,1:T(8,128)}, u32[]{:S(2)}) copy-start(f32[32,16,64]{2,0,1:T(8,128)} %copy-done.21) | copy-start | bytes 393220
  780.2 22.3 %copy-start.24 = (f32[32,16,64]{2,0,1:T(8,128)S(1)}, f32[32,16,64]{2,0,1:T(8,128)}, u32[]{:S(2)}) copy-start(f32[32,16,64]{2,0,1:T(8,128)} %copy-done.23) | copy-start | bytes 393220
  780.5 6.7 collective-permute-start.25
  782.5 5.8 collective-permute-start.24
  788.5 12.3 %collective-permute-start.26 = (f32[19,34,1,64]{3,1,2,0:T(8,128)S(1)}, f32[19,34,1,64]{3,1,2,0:T(8,128)S(1)}, u32[]{:S(2)}, u32[]{:S(2)}) collective-permute-start(f32[19,34,1,64]{3,1,2,0:T(8,128)S(1)} %get-tuple-element.40), channel_id=1, source_target_pairs={{1,0},{2,1},{3,2},{4,3},{5,4},{6,5},{7,6},{8,7},{9,8},{10,9},{11,1... | collective-permute-start | bytes 496136 | tf_op jit(solution)/shard_map/ppermute | solution.py:38
  789.8 12.7 %collective-permute-start.27 = (f32[19,34,1,64]{3,1,2,0:T(8,128)S(1)}, f32[19,34,1,64]{3,1,2,0:T(8,128)S(1)}, u32[]{:S(2)}, u32[]{:S(2)}) collective-permute-start(f32[19,34,1,64]{3,1,2,0:T(8,128)S(1)} %get-tuple-element.41), channel_id=1, source_target_pairs={{0,1},{1,2},{2,3},{3,4},{4,5},{5,6},{6,7},{7,8},{8,9},{9,10},{10,1... | collective-permute-start | bytes 496136 | tf_op jit(solution)/shard_map/ppermute | solution.py:36
  850.6 38.0 %copy-start.35 = (f32[32,16,64]{2,0,1:T(8,128)S(1)}, f32[32,16,64]{2,0,1:T(8,128)}, u32[]{:S(2)}) copy-start(f32[32,16,64]{2,0,1:T(8,128)} %get-tuple-element.80) | copy-start | bytes 393220
  850.6 81.4 %all-to-all-start.2 = ((f32[19,32,1024]{2,0,1:T(8,128)}), f32[19,32,1024]{2,0,1:T(8,128)S(1)}, u32[]{:S(2)}, u32[]{:S(2)}) async-start(f32[19,32,1024]{2,0,1:T(8,128)} %reshape.141), calls=%async_computation.2 | async-start | bytes 6291456 | tf_op jit(solution)/shard_map/all_to_all | solution.py:197
  (15 other events, 47.4 us)
where the time goes:
time: 954 us; the launch traced here: 940 us
  other arithmetic  480 us (50%)
  local copies, waits for them, and re-layouts  194 us (20%)
  starting transfers between devices  150 us (16%)
  waiting for transfers between devices  82.1 us (9%)
  matrix products  33 us (3%)
    add x1, other arithmetic, light_profile(): extinct = water_extinction + pigment_extinction * pigment  245 us
    unnamed x1, other arithmetic  146 us
    unnamed x100, local copies, waits for them, and re-layouts  80.8 us
    ppermute x14, starting transfers between devices, with_halo(): lax.ppermute(tail, axis, [(i, (i + 1) % count) for i in range(ends)])  67.2 us
    div x4, other arithmetic, react_tracers(): saturated = advected / (saturation + jnp.abs(advected))  41.9 us
    all_to_all x1, starting transfers between devices, shards(): lax.all_to_all(stocks.reshape(tracer_count, rows_tile, columns_tile * lev...  38 us
    ppermute x14, waiting for transfers between devices, with_halo(): lax.ppermute(head, axis, [((i + 1) % count, i) for i in range(ends)])  37.9 us
    all_to_all x1, waiting for transfers between devices, shards(): lax.all_to_all(stocks.reshape(tracer_count, rows_tile, columns_tile * lev...  33.9 us
  transfers between devices with their start and end apart: 31, of which 17 were waited for; matrix products, arithmetic and copies ran while one was open for 25% of the time, Pallas kernels for 0%

commit v1 on v0

v1 whole, which is shorter than its diff:
```python
import jax
import jax.numpy as jnp
from jax import lax
from jax.experimental import pallas as pl
from jax.experimental.pallas import tpu as pltpu
from jax.sharding import PartitionSpec as P

NC = 2
NB = 2
HALO = NC * NB

courant = 0.2
diffusion = 0.08
viscosity = 0.08
time_step = 0.1
thermal = 0.2
haline = 0.15
gravity = 0.1
coriolis = 0.5
coriolis_slope = 0.5
water_extinction = 0.04
pigment_extinction = 0.01
heating_rate = 0.5
light_half = 0.3
warming = 0.1
saturation = 0.5
reaction = 0.5

LANES = 128
ROWS8 = 8
F32 = jnp.float32
BF16 = jnp.bfloat16


def window_kernel(strip, depth_plane, out, big, sem_in, sem_out):
    planes, lines = big.shape[0], strip.shape[1]
    tiles, wide = out.shape[0], out.shape[2]
    step = lines // tiles
    edge = (wide - step) // 2
    tracers_in = pltpu.make_async_copy(strip, big.at[pl.ds(0, planes - 1), pl.ds(edge, lines)], sem_in.at[0])
    depth_in = pltpu.make_async_copy(depth_plane, big.at[pl.ds(planes - 1, 1), pl.ds(edge, lines)], sem_in.at[1])
    tracers_in.start()
    depth_in.start()
    zeros = jnp.zeros((planes, edge, 1, LANES), F32)
    big[:, pl.ds(0, edge)] = zeros
    big[:, pl.ds(edge + lines, edge)] = zeros
    tracers_in.wait()
    depth_in.wait()

    def send(d):
        return pltpu.make_async_copy(big.at[:, pl.ds(d * step, wide)], out.at[d], sem_out.at[d])

    @pl.loop(0, tiles)
    def _(d):
        send(d).start()

    @pl.loop(0, tiles)
    def _(d):
        send(d).wait()


def cut_windows(strip, depth_plane, tiles, wide):
    planes = strip.shape[0] + 1
    lines = strip.shape[1]
    edge = (wide - lines // tiles) // 2
    anywhere = pl.BlockSpec(memory_space=pl.ANY)
    return pl.pallas_call(
        window_kernel,
        out_shape=jax.ShapeDtypeStruct((tiles, planes, wide, 1, LANES), F32),
        in_specs=[anywhere, anywhere],
        out_specs=anywhere,
        scratch_shapes=[
            pltpu.VMEM((planes, lines + 2 * edge, 1, LANES), F32),
            pltpu.SemaphoreType.DMA((2,)),
            pltpu.SemaphoreType.DMA((tiles,)),
        ],
        name="cut_windows",
    )(strip, depth_plane)


def main_kernel(
    tile, south, north, ocean, ocean_south, ocean_north, mix_ref, ocean_out, out,
    raw, stock_a, stock_b, sea, ocean_a, ocean_b, press, wet, weights, growth0, result, sem,
):
    ntr = stock_a.shape[2]
    ncp, nrt = stock_a.shape[0], stock_a.shape[1]
    planes = ntr + 1
    line_stride = planes * ncp
    rows = tile.shape[0] // line_stride
    halo = HALO
    inner = ncp - halo
    copies = [
        pltpu.make_async_copy(south, raw.at[pl.ds(0, halo * line_stride)], sem.at[0]),
        pltpu.make_async_copy(tile, raw.at[pl.ds(halo * line_stride, rows * line_stride)], sem.at[1]),
        pltpu.make_async_copy(north, raw.at[pl.ds((halo + rows) * line_stride, halo * line_stride)], sem.at[2]),
    ]
    for copy in copies:
        copy.start()

    lane = lax.broadcasted_iota(jnp.int32, (ROWS8, LANES), 1)
    sub = lax.broadcasted_iota(jnp.int32, (ROWS8, LANES), 0)
    half = LANES // 2
    level = lane % half
    left = lane < half
    level_f = level.astype(F32)

    def roll_lanes(x, by):
        return pltpu.roll(x, by, x.ndim - 1)

    def roll_rows(x, by):
        return pltpu.roll(x, by, x.ndim - 2)

    def running_sum(x):
        by = 1
        while by < half:
            x = x + jnp.where(level >= by, roll_lanes(x, by), 0.0)
            by *= 2
        return x

    def around(ref, cp, rt, *more):
        up = ref[(cp, jnp.minimum(rt + 1, nrt - 1), *more)]
        down = ref[(cp, jnp.maximum(rt - 1, 0), *more)]
        right = ref[(jnp.minimum(cp + 1, ncp - 1), rt, *more)]
        leftward = ref[(jnp.maximum(cp - 1, 0), rt, *more)]
        centre = ref[(cp, rt, *more)]
        cell_north = roll_rows(jnp.where(sub == 0, up, centre), ROWS8 - 1)
        cell_south = roll_rows(jnp.where(sub == ROWS8 - 1, down, centre), 1)
        swapped = roll_lanes(centre, half)
        far = roll_lanes(jnp.where(left, right, leftward), half)
        return centre, swapped, far, cell_north, cell_south

    def five(ref, cp, rt, *more):
        centre, swapped, far, cell_north, cell_south = around(ref, cp, rt, *more)
        return centre, jnp.where(left, swapped, far), jnp.where(left, far, swapped), cell_north, cell_south

    for f in range(4):
        sea[f, pl.ds(0, halo), :] = ocean_south[f]
        sea[f, pl.ds(halo, rows), :] = ocean[f]
        sea[f, pl.ds(halo + rows, halo), :] = ocean_north[f]
    for cp in range(ncp):
        for f in range(4):
            for rt in range(nrt):
                ocean_a[cp, rt, f] = sea[f, pl.ds(rt * ROWS8, ROWS8), pl.ds(cp * LANES, LANES)]

    wide = ntr * ROWS8
    pick = (lax.broadcasted_iota(jnp.int32, (wide, ntr), 0) // ROWS8 == lax.broadcasted_iota(jnp.int32, (wide, ntr), 1)).astype(F32)
    pick_t = (lax.broadcasted_iota(jnp.int32, (ntr, wide), 1) // ROWS8 == lax.broadcasted_iota(jnp.int32, (ntr, wide), 0)).astype(F32)
    spread = jnp.dot(
        jnp.dot(pick, mix_ref[...], precision=lax.Precision.HIGHEST, preferred_element_type=F32),
        pick_t, precision=lax.Precision.HIGHEST, preferred_element_type=F32,
    )
    same = lax.broadcasted_iota(jnp.int32, (wide, wide), 0) % ROWS8 == lax.broadcasted_iota(jnp.int32, (wide, wide), 1) % ROWS8
    spread = jnp.where(same, spread, 0.0)
    mix_hi = spread.astype(BF16)
    mix_lo = (spread - mix_hi.astype(F32)).astype(BF16)

    for copy in copies:
        copy.wait()

    @pl.loop(0, ncp)
    def _(cp):
        for rt in range(nrt):
            base = rt * ROWS8 * line_stride + cp
            for t in range(ntr):
                stock_a[cp, rt, t] = raw[pl.ds(base + t * ncp, ROWS8, stride=line_stride), :]
            depth = raw[pl.ds(base + ntr * ncp, ROWS8, stride=line_stride), :]
            wet[cp, rt] = (level_f < depth).astype(F32)

    first_row = lax.axis_index("grp") * rows - halo
    total_rows = rows * lax.axis_size("grp")

    def ocean_step(old, new, stock):
        @pl.loop(0, ncp)
        def _(cp):
            for rt in range(nrt):
                density = (haline * old[cp, rt, 3] - thermal * old[cp, rt, 2]) * wet[cp, rt]
                press[cp, rt] = gravity * running_sum(density)

        @pl.loop(0, ncp)
        def _(cp):
            @pl.loop(0, nrt)
            def _(rt):
                w = five(wet, cp, rt)
                open_e, open_w, open_n, open_s = (w[0] * w[k] for k in range(1, 5))
                u = five(old, cp, rt, 0)
                v = five(old, cp, rt, 1)
                temp = five(old, cp, rt, 2)
                salt = five(old, cp, rt, 3)
                p = five(press, cp, rt)
                fe = 0.5 * (u[0] + u[1]) * open_e
                fw = 0.5 * (u[0] + u[2]) * open_w
                fn = 0.5 * (v[0] + v[3]) * open_n
                fs = 0.5 * (v[0] + v[4]) * open_s
                slope_x = 0.5 * (open_e * (p[1] - p[0]) + open_w * (p[0] - p[2]))
                slope_y = 0.5 * (open_n * (p[3] - p[0]) + open_s * (p[0] - p[4]))
                row = (first_row + rt * ROWS8 + sub).astype(F32)
                f = coriolis + coriolis_slope * ((row + 0.5) / total_rows - 0.5)
                extinct = water_extinction + pigment_extinction * stock[cp, rt, 0]
                irradiance = jnp.exp(-(running_sum(extinct) - 0.5 * extinct))
                heating = heating_rate * extinct * irradiance

                def lap(q):
                    return open_e * (q[1] - q[0]) + open_w * (q[2] - q[0]) + open_n * (q[3] - q[0]) + open_s * (q[4] - q[0])

                we = -courant * jnp.minimum(fe, 0.0)
                ww = courant * jnp.maximum(fw, 0.0)
                wn = -courant * jnp.minimum(fn, 0.0)
                ws = courant * jnp.maximum(fs, 0.0)
                wc = 1.0 - courant * (
                    jnp.maximum(fe, 0.0) - jnp.minimum(fw, 0.0) + jnp.maximum(fn, 0.0) - jnp.minimum(fs, 0.0)
                )

                def carried(q):
                    return wc * q[0] + we * q[1] + ww * q[2] + wn * q[3] + ws * q[4]

                weights[cp, rt, 0] = wc
                weights[cp, rt, 1] = jnp.where(left, we, ww)
                weights[cp, rt, 2] = jnp.where(left, ww, we)
                weights[cp, rt, 3] = wn
                weights[cp, rt, 4] = ws
                new[cp, rt, 0] = (u[0] + time_step * (f * v[0] - slope_x) + viscosity * lap(u)) * w[0]
                new[cp, rt, 1] = (v[0] + time_step * (-f * u[0] - slope_y) + viscosity * lap(v)) * w[0]
                warm = (carried(temp) + diffusion * lap(temp) + heating) * w[0]
                new[cp, rt, 2] = warm
                new[cp, rt, 3] = (carried(salt) + diffusion * lap(salt)) * w[0]
                growth0[cp, rt] = reaction * jnp.exp(warming * warm) * w[0]

    def tile_step(old, cp, rt):
        wc, wx, wz, wn, ws = (weights[cp, rt, k] for k in range(5))
        advected = []
        saturated = []
        for t in range(ntr):
            c, x, z, n, s = around(old, cp, rt, t)
            a = wc * c + wx * x + wz * z + wn * n + ws * s
            advected.append(a)
            saturated.append(a / (saturation + jnp.abs(a)))
        extinct = water_extinction + pigment_extinction * advected[0]
        irradiance = jnp.exp(-(running_sum(extinct) - 0.5 * extinct))
        growth = irradiance / (irradiance + light_half) * growth0[cp, rt]
        return advected, jnp.concatenate(saturated, axis=0), growth

    def substep(old, first, last, put):
        @pl.loop(0, (last - first) // 2)
        def _(k):
            cp = first + 2 * k

            @pl.loop(0, nrt)
            def _(rt):
                a0, s0, g0 = tile_step(old, cp, rt)
                a1, s1, g1 = tile_step(old, cp + 1, rt)
                s = jnp.concatenate([s0, s1], axis=1)
                s_hi = s.astype(BF16)
                s_lo = (s - s_hi.astype(F32)).astype(BF16)
                mixed = (
                    jnp.dot(mix_hi, s_hi, preferred_element_type=F32)
                    + jnp.dot(mix_hi, s_lo, preferred_element_type=F32)
                    + jnp.dot(mix_lo, s_hi, preferred_element_type=F32)
                )
                for t in range(ntr):
                    block = mixed[t * ROWS8:(t + 1) * ROWS8]
                    put(cp, rt, t, a0[t] + g0 * block[:, :LANES])
                    put(cp + 1, rt, t, a1[t] + g1 * block[:, LANES:])

    def put_in(ref):
        def put(cp, rt, t, value):
            ref[cp, rt, t] = value

        return put

    def put_out(cp, rt, t, value):
        start = rt * ROWS8 * (ntr * inner) + t * inner + (cp - halo // 2)
        result[pl.ds(start, ROWS8, stride=ntr * inner), :] = value

    edge = halo // 2
    ocean_step(ocean_a, ocean_b, stock_a)
    substep(stock_a, 0, ncp, put_in(stock_b))
    substep(stock_b, 0, ncp, put_in(stock_a))
    ocean_step(ocean_b, ocean_a, stock_a)
    substep(stock_a, 0, ncp, put_in(stock_b))
    substep(stock_b, edge, ncp - edge, put_out)
    send = pltpu.make_async_copy(result.at[pl.ds(halo * ntr * inner, rows * ntr * inner)], out, sem.at[0])
    send.start()
    for f in range(4):
        for cp in range(inner):
            for rt in range(nrt):
                sea[f, pl.ds(rt * ROWS8, ROWS8), pl.ds(cp * LANES, LANES)] = ocean_a[cp + edge, rt, f]
        ocean_out[f] = sea[f, pl.ds(halo, rows), pl.ds(0, inner * LANES)]
    send.wait()


def run_window(tile, south, north, ocean, ocean_south, ocean_north, interaction, ntr, ncp):
    rows = ocean.shape[1]
    halo = HALO
    nrt = (rows + 2 * halo) // ROWS8
    inner = ncp - halo
    anywhere = pl.BlockSpec(memory_space=pl.ANY)
    inside = pl.BlockSpec(memory_space=pltpu.VMEM)
    return pl.pallas_call(
        main_kernel,
        out_shape=(
            jax.ShapeDtypeStruct((4, rows, inner * LANES), F32),
            jax.ShapeDtypeStruct((rows * ntr * inner, LANES), F32),
        ),
        in_specs=[anywhere] * 3 + [inside] * 4,
        out_specs=(inside, anywhere),
        scratch_shapes=[
            pltpu.VMEM(((rows + 2 * halo) * (ntr + 1) * ncp, LANES), F32),
            pltpu.VMEM((ncp, nrt, ntr, ROWS8, LANES), F32),
            pltpu.VMEM((ncp, nrt, ntr, ROWS8, LANES), F32),
            pltpu.VMEM((4, rows + 2 * halo, ncp * LANES), F32),
            pltpu.VMEM((ncp, nrt, 4, ROWS8, LANES), F32),
            pltpu.VMEM((ncp, nrt, 4, ROWS8, LANES), F32),
            pltpu.VMEM((ncp, nrt, ROWS8, LANES), F32),
            pltpu.VMEM((ncp, nrt, ROWS8, LANES), F32),
            pltpu.VMEM((ncp, nrt, 5, ROWS8, LANES), F32),
            pltpu.VMEM((ncp, nrt, ROWS8, LANES), F32),
            pltpu.VMEM(((rows + 2 * halo) * ntr * inner, LANES), F32),
            pltpu.SemaphoreType.DMA((3,)),
        ],
        name="window",
    )(tile, south, north, ocean, ocean_south, ocean_north, interaction)


def shift(array, axis, by):
    count = lax.axis_size(axis)
    if by > 0:
        return lax.ppermute(array, axis, [(i, i + 1) for i in range(count - 1)])
    return lax.ppermute(array, axis, [(i + 1, i) for i in range(count - 1)])


def shards(ocean_fields, tracers, wet_levels, interaction):
    tiles = lax.axis_size("gx")
    ntr = tracers.shape[0]
    rows = ocean_fields.shape[1]
    columns = wet_levels.shape[1]
    levels = tracers.shape[2] // columns
    lines = tracers.shape[2] // LANES
    pair = LANES // levels
    inner = lines // tiles
    edge = HALO // pair
    ncp = inner + 2 * edge
    planes = ntr + 1

    margin = edge * LANES
    from_west = shift(ocean_fields[:, :, -margin:], "gx", 1)
    from_east = shift(ocean_fields[:, :, :margin], "gx", -1)
    depth = jnp.broadcast_to(wet_levels.astype(F32).reshape(lines, pair, 1), (lines, pair, levels))
    sent = cut_windows(tracers.reshape(ntr, lines, 1, LANES), depth.reshape(1, lines, 1, LANES), tiles, ncp)
    ocean = jnp.concatenate([from_west, ocean_fields, from_east], axis=2)
    ocean_south = shift(ocean[:, -HALO:], "grp", 1)
    ocean_north = shift(ocean[:, :HALO], "grp", -1)
    sent, ocean, ocean_south, ocean_north = lax.optimization_barrier((sent, ocean, ocean_south, ocean_north))
    tile = lax.all_to_all(sent.reshape(tiles, planes * ncp, LANES), "gx", split_axis=0, concat_axis=0, tiled=True)
    south = shift(tile[-HALO:], "grp", 1)
    north = shift(tile[:HALO], "grp", -1)
    ocean_next, result = run_window(
        tile.reshape(-1, LANES), south.reshape(-1, LANES), north.reshape(-1, LANES),
        ocean, ocean_south, ocean_north, interaction, ntr, ncp,
    )
    back = lax.all_to_all(result.reshape(tiles, ntr * inner, LANES), "gx", split_axis=0, concat_axis=0, tiled=True)
    back = back.reshape(tiles, ntr, inner, LANES).transpose(1, 0, 2, 3)
    return ocean_next, back.reshape(ntr, 1, lines * LANES)


def solution(mesh):
    placed = (P(None, "grp", "gx"), P(None, ("grp", "gx"), None), P(("grp", "gx"), None), P())
    return jax.shard_map(
        shards,
        mesh=mesh,
        in_specs=placed,
        out_specs=(P(None, "grp", "gx"), P(None, ("grp", "gx"), None)),
        check_vma=False,
    )
```

time: 954 us -> 270 us (0.28); the launches traced: 940 us -> 269 us
  other arithmetic: 480 us -> 0.02 us
  local copies, waits for them, and re-layouts: 194 us -> 7.55 us
  Pallas kernels: 0 us -> 137 us
  starting transfers between devices: 150 us -> 18 us
  blocking collectives: 0 us -> 96.5 us
  waiting for transfers between devices: 82.1 us -> 9.07 us
  matrix products: 33 us -> 0 us
    add x6 -> x0, other arithmetic: 270 us -> none  [the longest x1 245 us: light_profile(): extinct = water_extinction + pigment_extinction * pigment]
    unnamed x1 -> x0, other arithmetic: 146 us -> none
    pallas_call x0 -> x2, Pallas kernels: none -> 137 us  [the longest x1 133 us: run_window(): pl.pallas_call(main_kernel, out_shape=(jax.ShapeDtypeStruct((4, rows, inn...]
    all_to_all x0 -> x2, blocking collectives: none -> 96.5 us  [the longest x1 61 us: shards(): lax.all_to_all(sent.reshape(tiles, planes * ncp, LANES), 'gx', split_axis...]
    unnamed x100 -> x16, local copies, waits for them, and re-layouts: 80.8 us -> 3.74 us
    ppermute x28 -> x6, starting transfers between devices: 90 us -> 18 us  [the longest x3 9 us: shift(): return lax.ppermute(array, axis, [(i + 1, i) for i in range(count - 1)])]
    reshape x13 -> x2, local copies, waits for them, and re-layouts: 65.6 us -> 2.47 us  [the longest x1 1.72 us: shards(): back = back.reshape(tiles, ntr, inner, LANES).transpose(1, 0, 2, 3)]
    all_to_all x3 -> x0, starting transfers between devices: 59.6 us -> none  [the longest x1 38 us: shards(): lax.all_to_all(stocks.reshape(tracer_count, rows_tile, columns_tile * lev...]
  transfers between devices with their start and end apart: 31 -> 6, of which waited for: 17 -> 4; matrix products, arithmetic and copies ran while one was open for 25% -> 1% of each run, Pallas kernels for 0% -> 1%
where the time goes in v1:
time: 270 us; the launch traced here: 269 us
  Pallas kernels  137 us (51%)
  blocking collectives  96.5 us (36%)
  starting transfers between devices  18 us (7%)
  waiting for transfers between devices  9.07 us (3%)
  local copies, waits for them, and re-layouts  7.55 us (3%)
    pallas_call x1, Pallas kernels, run_window(): pl.pallas_call(main_kernel, out_shape=(jax.ShapeDtypeStruct((4, rows, inn...  133 us
    all_to_all x1, blocking collectives, shards(): lax.all_to_all(sent.reshape(tiles, planes * ncp, LANES), 'gx', split_axis...  61 us
    all_to_all x1, blocking collectives, shards(): lax.all_to_all(result.reshape(tiles, ntr * inner, LANES), 'gx', split_axi...  35.4 us
    ppermute x3, starting transfers between devices, shift(): return lax.ppermute(array, axis, [(i + 1, i) for i in range(count - 1)])  9 us
    ppermute x3, starting transfers between devices, shift(): return lax.ppermute(array, axis, [(i, i + 1) for i in range(count - 1)])  8.96 us
    ppermute x3, waiting for transfers between devices, shift(): return lax.ppermute(array, axis, [(i + 1, i) for i in range(count - 1)])  6.97 us
  transfers between devices with their start and end apart: 6, of which 4 were waited for; matrix products, arithmetic and copies ran while one was open for 1% of the time, Pallas kernels for 1%

profile of v1, /device:TPU:1, one launch (start us, length us, event | category | flops | bytes accessed | tf_op | source)
XLA Modules:
  0.0 269.1 jit_solution(17658998667687031948)
XLA Ops:
  0.6 0.0 copy-start.6
  0.6 1.0 fusion.2
  1.6 3.9 %collective-permute-start = (f32[4,32,256]{2,1,0:T(8,128)S(1)}, f32[4,32,256]{2,1,0:T(8,128)S(1)}, u32[]{:S(2)}, u32[]{:S(2)}) collective-permute-start(f32[4,32,256]{2,1,0:T(8,128)S(1)} %get-tuple-element.19), channel_id=1, source_target_pairs={{0,1},{1,2},{2,3},{3,4},{4,5},{5,6},{6,7},{7,8},{8,9},{9,10},{10,1... | collective-permute-start | bytes 393224 | tf_op jit(solution)/shard_map/ppermute | solution.py:327
  5.6 1.3 collective-permute-start.1
  6.9 0.9 collective-permute-done
  7.8 1.1 constant_dynamic-update-slice_fusion.1
  8.8 2.5 collective-permute-done.1
  11.3 0.0 copy-start.1
  11.4 4.0 %collective-permute-start.3 = (f32[4,4,1536]{2,1,0:T(4,128)S(1)}, f32[4,4,1536]{2,1,0:T(4,128)S(1)}, u32[]{:S(2)}, u32[]{:S(2)}) collective-permute-start(f32[4,4,1536]{2,1,0:T(4,128)S(1)} %get-tuple-element.16), channel_id=1, source_target_pairs={{32,0},{64,32},{96,64},{33,1},{65,33},{97,65},{34,2},{66,34},{98,6... | collective-permute-start | bytes 294920 | tf_op jit(solution)/shard_map/ppermute | solution.py:328
  15.4 3.1 %collective-permute-start.2 = (f32[4,4,1536]{2,1,0:T(4,128)S(1)}, f32[4,4,1536]{2,1,0:T(4,128)S(1)}, u32[]{:S(2)}, u32[]{:S(2)}) collective-permute-start(f32[4,4,1536]{2,1,0:T(4,128)S(1)} %get-tuple-element.17), channel_id=1, source_target_pairs={{0,32},{32,64},{64,96},{1,33},{33,65},{65,97},{2,34},{34,66},{66,9... | collective-permute-start | bytes 294920 | tf_op jit(solution)/shard_map/ppermute | solution.py:327
  18.5 0.0 copy-done.6
  18.5 0.1 broadcast_in_dim.7
  18.7 0.1 copy.7
  18.8 0.8 copy.8.depth_plane
  19.5 3.9 %cut_windows.1 = f32[32,20,12,1,128]{4,3,2,1,0:T(1,128)} custom-call(f32[19,256,1,128]{3,2,1,0:T(1,128)} %bitcast.14, f32[1,256,1,128]{3,2,1,0:T(1,128)} %copy.8.depth_plane), custom_call_target="tpu_custom_call" | custom-call | tf_op jit(solution)/shard_map/cut_windows/pallas_call | solution.py:67
  23.4 0.0 copy-done.1
  23.4 0.0 collective-permute-done.3.ocean_north
  23.4 0.0 copy-start.4
  23.4 0.0 collective-permute-done.2.ocean_south
  23.4 0.0 copy-start.5
  23.4 61.0 %all_to_all.10 = f32[32,240,128]{2,1,0:T(8,128)S(1)} all-to-all(f32[32,240,128]{2,1,0:T(8,128)} %bitcast.12), channel_id=1, replica_groups=mesh['grp'=4,'gx'=32] {'gx'}, dimensions={0} | all-to-all | bytes 7864320 | tf_op jit(solution)/shard_map/all_to_all | solution.py:353
  84.5 0.0 copy-done.4
  84.5 0.0 copy-done.5
  84.5 0.0 copy-start
  84.5 1.9 copy-done
  86.3 0.1 fusion
  86.4 3.7 %collective-permute-start.5 = (f32[4,240,128]{2,1,0:T(8,128)S(1)}, f32[4,240,128]{2,1,0:T(8,128)S(1)}, u32[]{:S(2)}, u32[]{:S(2)}) collective-permute-start(f32[4,240,128]{2,1,0:T(8,128)S(1)} %get-tuple-element.14), channel_id=1, source_target_pairs={{32,0},{64,32},{96,64},{33,1},{65,33},{97,65},{34,2},{66,34},{98,6... | collective-permute-start | bytes 1474568 | tf_op jit(solution)/shard_map/ppermute | solution.py:328
  90.1 1.9 collective-permute-start.4
  92.0 4.5 %collective-permute-done.5 = f32[4,240,128]{2,1,0:T(8,128)S(1)} collective-permute-done((f32[4,240,128]{2,1,0:T(8,128)S(1)}, f32[4,240,128]{2,1,0:T(8,128)S(1)}, u32[]{:S(2)}, u32[]{:S(2)}) %collective-permute-start.5) | collective-permute-done | bytes 491552 | tf_op jit(solution)/shard_map/ppermute | solution.py:328
  96.6 0.0 copy-start.2
  96.6 1.2 collective-permute-done.4
  97.8 0.0 copy-start.3
  97.8 0.0 copy-done.2
  97.8 0.8 copy-done.3
  98.6 133.3 %window.1 = (f32[4,32,1024]{2,1,0:T(8,128)}, f32[4864,128]{1,0:T(8,128)}) custom-call(f32[7680,128]{1,0:T(8,128)} %bitcast.11, f32[960,128]{1,0:T(8,128)} %bitcast.19, f32[960,128]{1,0:T(8,128)} %bitcast.18, f32[4,32,1536]{2,1,0:T(8,128)} %copy-done.1, f32[4,4,1536]{2,1,0:T(4,128)} %copy-done.5, f32[4,4,1536]{2,1,0:T(4,128)} %copy-done.4, f32[19,19]{1,0:T(8,128)} %mix_ref.1), custom_call_target="tpu_custom_call" | custom-call | tf_op jit(solution)/shard_map/window/pallas_call | solution.py:298
  231.9 35.4 %all_to_all.11 = f32[32,152,128]{2,1,0:T(8,128)S(1)} all-to-all(f32[32,152,128]{2,1,0:T(8,128)} %bitcast.15), channel_id=1, replica_groups=mesh['grp'=4,'gx'=32] {'gx'}, dimensions={0} | all-to-all | bytes 4980736 | tf_op jit(solution)/shard_map/all_to_all | solution.py:360
  267.3 1.7 copy.9
  (5 shorter events, 0.1 us)
Async XLA Ops:
  0.6 17.9 %copy-start.6 = (s32[1,512]{1,0:T(1,128)S(1)}, s32[1,512]{1,0:T(1,128)}, u32[]{:S(2)}) copy-start(s32[1,512]{1,0:T(1,128)} %param.6) | copy-start | bytes 6148
  1.6 6.1 %collective-permute-start = (f32[4,32,256]{2,1,0:T(8,128)S(1)}, f32[4,32,256]{2,1,0:T(8,128)S(1)}, u32[]{:S(2)}, u32[]{:S(2)}) collective-permute-start(f32[4,32,256]{2,1,0:T(8,128)S(1)} %get-tuple-element.19), channel_id=1, source_target_pairs={{0,1},{1,2},{2,3},{3,4},{4,5},{5,6},{6,7},{7,8},{8,9},{9,10},{10,1... | collective-permute-start | bytes 393224 | tf_op jit(solution)/shard_map/ppermute | solution.py:327
  5.6 5.7 %collective-permute-start.1 = (f32[4,32,256]{2,1,0:T(8,128)S(1)}, f32[4,32,256]{2,1,0:T(8,128)S(1)}, u32[]{:S(2)}, u32[]{:S(2)}) collective-permute-start(f32[4,32,256]{2,1,0:T(8,128)S(1)} %get-tuple-element.18), channel_id=1, source_target_pairs={{1,0},{2,1},{3,2},{4,3},{5,4},{6,5},{7,6},{8,7},{9,8},{10,9},{11,1... | collective-permute-start | bytes 393224 | tf_op jit(solution)/shard_map/ppermute | solution.py:328
  11.3 12.1 %copy-start.1 = (f32[4,32,1536]{2,1,0:T(8,128)}, f32[4,32,1536]{2,1,0:T(8,128)S(1)}, u32[]{:S(2)}) copy-start(f32[4,32,1536]{2,1,0:T(8,128)S(1)} %constant_dynamic-update-slice_fusion.ocean) | copy-start | bytes 2359300
  11.4 12.0 %collective-permute-start.3 = (f32[4,4,1536]{2,1,0:T(4,128)S(1)}, f32[4,4,1536]{2,1,0:T(4,128)S(1)}, u32[]{:S(2)}, u32[]{:S(2)}) collective-permute-start(f32[4,4,1536]{2,1,0:T(4,128)S(1)} %get-tuple-element.16), channel_id=1, source_target_pairs={{32,0},{64,32},{96,64},{33,1},{65,33},{97,65},{34,2},{66,34},{98,6... | collective-permute-start | bytes 294920 | tf_op jit(solution)/shard_map/ppermute | solution.py:328
  15.4 8.0 %collective-permute-start.2 = (f32[4,4,1536]{2,1,0:T(4,128)S(1)}, f32[4,4,1536]{2,1,0:T(4,128)S(1)}, u32[]{:S(2)}, u32[]{:S(2)}) collective-permute-start(f32[4,4,1536]{2,1,0:T(4,128)S(1)} %get-tuple-element.17), channel_id=1, source_target_pairs={{0,32},{32,64},{64,96},{1,33},{33,65},{65,97},{2,34},{34,66},{66,9... | collective-permute-start | bytes 294920 | tf_op jit(solution)/shard_map/ppermute | solution.py:327
  23.4 61.1 %copy-start.4 = (f32[4,4,1536]{2,1,0:T(4,128)}, f32[4,4,1536]{2,1,0:T(4,128)S(1)}, u32[]{:S(2)}) copy-start(f32[4,4,1536]{2,1,0:T(4,128)S(1)} %collective-permute-done.3.ocean_north) | copy-start | bytes 294916
  23.4 61.1 %copy-start.5 = (f32[4,4,1536]{2,1,0:T(4,128)}, f32[4,4,1536]{2,1,0:T(4,128)S(1)}, u32[]{:S(2)}) copy-start(f32[4,4,1536]{2,1,0:T(4,128)S(1)} %collective-permute-done.2.ocean_south) | copy-start | bytes 294916
  84.5 1.9 copy-start
  86.4 10.1 %collective-permute-start.5 = (f32[4,240,128]{2,1,0:T(8,128)S(1)}, f32[4,240,128]{2,1,0:T(8,128)S(1)}, u32[]{:S(2)}, u32[]{:S(2)}) collective-permute-start(f32[4,240,128]{2,1,0:T(8,128)S(1)} %get-tuple-element.14), channel_id=1, source_target_pairs={{32,0},{64,32},{96,64},{33,1},{65,33},{97,65},{34,2},{66,34},{98,6... | collective-permute-start | bytes 1474568 | tf_op jit(solution)/shard_map/ppermute | solution.py:328
  90.1 7.7 %collective-permute-start.4 = (f32[4,240,128]{2,1,0:T(8,128)S(1)}, f32[4,240,128]{2,1,0:T(8,128)S(1)}, u32[]{:S(2)}, u32[]{:S(2)}) collective-permute-start(f32[4,240,128]{2,1,0:T(8,128)S(1)} %get-tuple-element.15), channel_id=1, source_target_pairs={{0,32},{32,64},{64,96},{1,33},{33,65},{65,97},{2,34},{34,66},{66,9... | collective-permute-start | bytes 1474568 | tf_op jit(solution)/shard_map/ppermute | solution.py:327
  96.6 1.2 copy-start.2
  97.8 0.8 copy-start.3

commit v2 on v1

v2 whole, which is shorter than its diff:
```python
import jax
import jax.numpy as jnp
from jax import lax
from jax.experimental import pallas as pl
from jax.experimental.pallas import tpu as pltpu
from jax.sharding import PartitionSpec as P

NC = 2
NB = 2
HALO = NC * NB

courant = 0.2
diffusion = 0.08
viscosity = 0.08
time_step = 0.1
thermal = 0.2
haline = 0.15
gravity = 0.1
coriolis = 0.5
coriolis_slope = 0.5
water_extinction = 0.04
pigment_extinction = 0.01
heating_rate = 0.5
light_half = 0.3
warming = 0.1
saturation = 0.5
reaction = 0.5

LANES = 128
ROWS8 = 8
F32 = jnp.float32
BF16 = jnp.bfloat16


def window_kernel(strip, depth_plane, out, big, sem_in, sem_out):
    planes, lines = big.shape[0], strip.shape[1]
    tiles, wide = out.shape[0], out.shape[2]
    step = lines // tiles
    edge = (wide - step) // 2
    tracers_in = pltpu.make_async_copy(strip, big.at[pl.ds(0, planes - 1), pl.ds(edge, lines)], sem_in.at[0])
    depth_in = pltpu.make_async_copy(depth_plane, big.at[pl.ds(planes - 1, 1), pl.ds(edge, lines)], sem_in.at[1])
    tracers_in.start()
    depth_in.start()
    zeros = jnp.zeros((planes, edge, 1, LANES), F32)
    big[:, pl.ds(0, edge)] = zeros
    big[:, pl.ds(edge + lines, edge)] = zeros
    tracers_in.wait()
    depth_in.wait()

    def send(d):
        return pltpu.make_async_copy(big.at[:, pl.ds(d * step, wide)], out.at[d], sem_out.at[d])

    @pl.loop(0, tiles)
    def _(d):
        send(d).start()

    @pl.loop(0, tiles)
    def _(d):
        send(d).wait()


def cut_windows(strip, depth_plane, tiles, wide):
    planes = strip.shape[0] + 1
    lines = strip.shape[1]
    edge = (wide - lines // tiles) // 2
    anywhere = pl.BlockSpec(memory_space=pl.ANY)
    return pl.pallas_call(
        window_kernel,
        out_shape=jax.ShapeDtypeStruct((tiles, planes, wide, 1, LANES), F32),
        in_specs=[anywhere, anywhere],
        out_specs=anywhere,
        scratch_shapes=[
            pltpu.VMEM((planes, lines + 2 * edge, 1, LANES), F32),
            pltpu.SemaphoreType.DMA((2,)),
            pltpu.SemaphoreType.DMA((tiles,)),
        ],
        name="cut_windows",
    )(strip, depth_plane)


def main_kernel(
    tile, south, north, ocean, ocean_south, ocean_north, mix_ref, ocean_out, out,
    raw, stock_a, stock_b, sea, ocean_a, ocean_b, press, wet, weights, growth0, growth, flat, result, sem,
):
    ncp, nrt, ntr = stock_a.shape[0], stock_a.shape[1] - 2, stock_a.shape[2]
    planes = ntr + 1
    line_stride = planes * ncp
    rows = tile.shape[0] // line_stride
    halo = HALO
    inner = ncp - halo
    copies = [
        pltpu.make_async_copy(south, raw.at[pl.ds(0, halo * line_stride)], sem.at[0]),
        pltpu.make_async_copy(tile, raw.at[pl.ds(halo * line_stride, rows * line_stride)], sem.at[1]),
        pltpu.make_async_copy(north, raw.at[pl.ds((halo + rows) * line_stride, halo * line_stride)], sem.at[2]),
    ]
    for copy in copies:
        copy.start()

    lane = lax.broadcasted_iota(jnp.int32, (ROWS8, LANES), 1)
    sub = lax.broadcasted_iota(jnp.int32, (ROWS8, LANES), 0)
    half = LANES // 2
    left = lane < half
    level_f = (lane % half).astype(F32)

    def swap(x):
        return pltpu.roll(x, half, 1)

    def put(ref, cp, q, value, *more):
        ref[(cp, q + 1, *more)] = value
        if q == 0:
            ref[(cp, nrt + 1, *more)] = pltpu.roll(value, ROWS8 - 1, 0)
        if q == nrt - 1:
            ref[(cp, 0, *more)] = pltpu.roll(value, 1, 0)

    def around(ref, cp, q, *more):
        right = ref[(jnp.minimum(cp + 1, ncp - 1), q + 1, *more)]
        leftward = ref[(jnp.maximum(cp - 1, 0), q + 1, *more)]
        centre = ref[(cp, q + 1, *more)]
        far = swap(jnp.where(left, right, leftward))
        return centre, swap(centre), far, ref[(cp, q + 2, *more)], ref[(cp, q, *more)]

    def five(ref, cp, q, *more):
        centre, swapped, far, cell_north, cell_south = around(ref, cp, q, *more)
        return centre, jnp.where(left, swapped, far), jnp.where(left, far, swapped), cell_north, cell_south

    row_id = lax.broadcasted_iota(jnp.int32, (LANES, LANES), 0)
    col_id = lax.broadcasted_iota(jnp.int32, (LANES, LANES), 1)
    upper = ((row_id <= col_id) & (row_id // half == col_id // half)).astype(F32).astype(BF16)

    def running_sums(x):
        high = x.astype(BF16)
        rest = x - high.astype(F32)
        middle = rest.astype(BF16)
        low = (rest - middle.astype(F32)).astype(BF16)
        return (
            jnp.dot(high, upper, preferred_element_type=F32)
            + jnp.dot(middle, upper, preferred_element_type=F32)
            + jnp.dot(low, upper, preferred_element_type=F32)
        )

    for f in range(4):
        for cp in range(ncp):
            across = pl.ds(cp * LANES, LANES)
            sea[f, cp, pl.ds(0, halo), :] = ocean_south[f, :, across]
            sea[f, cp, pl.ds(halo, rows), :] = ocean[f, :, across]
            sea[f, cp, pl.ds(halo + rows, halo), :] = ocean_north[f, :, across]
            for q in range(nrt):
                put(ocean_a, cp, q, sea[f, cp, pl.ds(q, ROWS8, stride=nrt), :], f)

    wide = ntr * ROWS8
    pick = (lax.broadcasted_iota(jnp.int32, (wide, ntr), 0) // ROWS8 == lax.broadcasted_iota(jnp.int32, (wide, ntr), 1)).astype(F32)
    deep = (ntr + 1) * ROWS8
    pick_t = (lax.broadcasted_iota(jnp.int32, (ntr, deep), 1) // ROWS8 == lax.broadcasted_iota(jnp.int32, (ntr, deep), 0)).astype(F32)
    spread = jnp.dot(
        jnp.dot(pick, mix_ref[...], precision=lax.Precision.HIGHEST, preferred_element_type=F32),
        pick_t, precision=lax.Precision.HIGHEST, preferred_element_type=F32,
    )
    same = lax.broadcasted_iota(jnp.int32, (wide, deep), 0) % ROWS8 == lax.broadcasted_iota(jnp.int32, (wide, deep), 1) % ROWS8
    spread = jnp.where(same, spread, 0.0)
    mix_hi = spread.astype(BF16).astype(F32)
    mix_all = jnp.concatenate([mix_hi, mix_hi, spread - mix_hi], axis=1).astype(BF16)

    for copy in copies:
        copy.wait()

    @pl.loop(0, ncp)
    def _(cp):
        for q in range(nrt):
            base = q * line_stride + cp
            for t in range(ntr):
                put(stock_a, cp, q, raw[pl.ds(base + t * ncp, ROWS8, stride=nrt * line_stride), :], t)
            depth = raw[pl.ds(base + ntr * ncp, ROWS8, stride=nrt * line_stride), :]
            put(wet, cp, q, (level_f < depth).astype(F32))

    first_row = lax.axis_index("grp") * rows - halo
    total_rows = rows * lax.axis_size("grp")

    def line(cp, q):
        return pl.ds((cp * nrt + q) * ROWS8, ROWS8)

    def ocean_step(old, new, stock):
        for cp in range(ncp):
            for q in range(nrt):
                flat[line(cp, q), :] = (haline * old[cp, q + 1, 3] - thermal * old[cp, q + 1, 2]) * wet[cp, q + 1]
        flat[...] = gravity * running_sums(flat[...])
        for cp in range(ncp):
            for q in range(nrt):
                put(press, cp, q, flat[line(cp, q), :])
        for cp in range(ncp):
            for q in range(nrt):
                flat[line(cp, q), :] = water_extinction + pigment_extinction * stock[cp, q + 1, 0]
        extinct_all = flat[...]
        flat[...] = heating_rate * extinct_all * jnp.exp(-(running_sums(extinct_all) - 0.5 * extinct_all))

        @pl.loop(0, ncp)
        def _(cp):
            for q in range(nrt):
                w = five(wet, cp, q)
                open_e, open_w, open_n, open_s = (w[0] * w[k] for k in range(1, 5))
                u = five(old, cp, q, 0)
                v = five(old, cp, q, 1)
                temp = five(old, cp, q, 2)
                salt = five(old, cp, q, 3)
                p = five(press, cp, q)
                fe = 0.5 * (u[0] + u[1]) * open_e
                fw = 0.5 * (u[0] + u[2]) * open_w
                fn = 0.5 * (v[0] + v[3]) * open_n
                fs = 0.5 * (v[0] + v[4]) * open_s
                slope_x = 0.5 * (open_e * (p[1] - p[0]) + open_w * (p[0] - p[2]))
                slope_y = 0.5 * (open_n * (p[3] - p[0]) + open_s * (p[0] - p[4]))
                row = (first_row + q + nrt * sub).astype(F32)
                f = coriolis + coriolis_slope * ((row + 0.5) / total_rows - 0.5)
                heating = flat[pl.ds(pl.multiple_of((cp * nrt + q) * ROWS8, ROWS8), ROWS8), :]

                def lap(x):
                    return open_e * (x[1] - x[0]) + open_w * (x[2] - x[0]) + open_n * (x[3] - x[0]) + open_s * (x[4] - x[0])

                we = -courant * jnp.minimum(fe, 0.0)
                ww = courant * jnp.maximum(fw, 0.0)
                wn = -courant * jnp.minimum(fn, 0.0)
                ws = courant * jnp.maximum(fs, 0.0)
                wc = 1.0 - courant * (
                    jnp.maximum(fe, 0.0) - jnp.minimum(fw, 0.0) + jnp.maximum(fn, 0.0) - jnp.minimum(fs, 0.0)
                )

                def carried(x):
                    return wc * x[0] + we * x[1] + ww * x[2] + wn * x[3] + ws * x[4]

                weights[cp, q, 0] = wc
                weights[cp, q, 1] = jnp.where(left, we, ww)
                weights[cp, q, 2] = jnp.where(left, ww, we)
                weights[cp, q, 3] = wn
                weights[cp, q, 4] = ws
                put(new, cp, q, (u[0] + time_step * (f * v[0] - slope_x) + viscosity * lap(u)) * w[0], 0)
                put(new, cp, q, (v[0] + time_step * (-f * u[0] - slope_y) + viscosity * lap(v)) * w[0], 1)
                warm = (carried(temp) + diffusion * lap(temp) + heating) * w[0]
                put(new, cp, q, warm, 2)
                put(new, cp, q, (carried(salt) + diffusion * lap(salt)) * w[0], 3)
                growth0[cp, q] = reaction * jnp.exp(warming * warm) * w[0]

    def carry(old, cp, q, t, weight):
        c, x, z, n, s = around(old, cp, q, t)
        return weight[0] * c + weight[1] * x + weight[2] * z + weight[3] * n + weight[4] * s

    def substep(old, first, last, finish):
        for cp in range(first, last):
            for q in range(nrt):
                p = carry(old, cp, q, 0, [weights[cp, q, k] for k in range(5)])
                flat[line(cp, q), :] = water_extinction + pigment_extinction * p
        span = pl.ds(first * nrt * ROWS8, (last - first) * nrt * ROWS8)
        extinct = flat[span, :]
        irradiance = jnp.exp(-(running_sums(extinct) - 0.5 * extinct))
        flat[span, :] = irradiance / (irradiance + light_half)
        for cp in range(first, last):
            for q in range(nrt):
                growth[cp, q] = flat[line(cp, q), :] * growth0[cp, q]

        blank = jnp.zeros((ROWS8, LANES), F32)

        @pl.loop(first, last)
        def _(cp):
            def begin(q):
                weight = [weights[cp, q, k] for k in range(5)]
                advected, high, low = [], [], []
                for t in range(ntr):
                    a = carry(old, cp, q, t, weight)
                    s = a / (saturation + jnp.abs(a))
                    h = s.astype(BF16).astype(F32)
                    advected.append(a)
                    high.append(h)
                    low.append(s - h)
                high = jnp.concatenate(high + [blank], axis=0).astype(BF16)
                low = jnp.concatenate(low + [blank], axis=0).astype(BF16)
                return advected, jnp.concatenate([high, low, high], axis=0)

            def end(group, begun):
                parts = [b[1] for b in begun]
                s = parts[0] if len(parts) == 1 else jnp.concatenate(parts, axis=1)
                mixed = jnp.dot(mix_all, s, preferred_element_type=F32)
                for k, q in enumerate(group):
                    g = growth[cp, q]
                    for t in range(ntr):
                        block = mixed[t * ROWS8:(t + 1) * ROWS8, k * LANES:(k + 1) * LANES]
                        finish(cp, q, t, begun[k][0][t] + g * block)

            for q in range(0, nrt, 2):
                group = list(range(q, min(q + 2, nrt)))
                end(group, [begin(r) for r in group])

    def finish_in(ref):
        def finish(cp, q, t, value):
            put(ref, cp, q, value, t)

        return finish

    def finish_out(cp, q, t, value):
        start = q * (ntr * inner) + t * inner + (cp - halo // 2)
        result[pl.ds(start, ROWS8, stride=nrt * ntr * inner), :] = value

    edge = halo // 2
    ocean_step(ocean_a, ocean_b, stock_a)
    substep(stock_a, 0, ncp, finish_in(stock_b))
    substep(stock_b, edge // 2, ncp - edge // 2, finish_in(stock_a))
    ocean_step(ocean_b, ocean_a, stock_a)
    substep(stock_a, edge // 2, ncp - edge // 2, finish_in(stock_b))
    substep(stock_b, edge, ncp - edge, finish_out)
    send = pltpu.make_async_copy(result.at[pl.ds(halo * ntr * inner, rows * ntr * inner)], out, sem.at[0])
    send.start()
    for f in range(4):
        for cp in range(inner):
            for q in range(nrt):
                sea[f, cp, pl.ds(q, ROWS8, stride=nrt), :] = ocean_a[cp + edge, q + 1, f]
            ocean_out[f, :, pl.ds(cp * LANES, LANES)] = sea[f, cp, pl.ds(halo, rows), :]
    send.wait()


def run_window(tile, south, north, ocean, ocean_south, ocean_north, interaction, ntr, ncp):
    rows = ocean.shape[1]
    halo = HALO
    nrt = (rows + 2 * halo) // ROWS8
    inner = ncp - halo
    anywhere = pl.BlockSpec(memory_space=pl.ANY)
    inside = pl.BlockSpec(memory_space=pltpu.VMEM)
    return pl.pallas_call(
        main_kernel,
        out_shape=(
            jax.ShapeDtypeStruct((4, rows, inner * LANES), F32),
            jax.ShapeDtypeStruct((rows * ntr * inner, LANES), F32),
        ),
        in_specs=[anywhere] * 3 + [inside] * 4,
        out_specs=(inside, anywhere),
        scratch_shapes=[
            pltpu.VMEM(((rows + 2 * halo) * (ntr + 1) * ncp, LANES), F32),
            pltpu.VMEM((ncp, nrt + 2, ntr, ROWS8, LANES), F32),
            pltpu.VMEM((ncp, nrt + 2, ntr, ROWS8, LANES), F32),
            pltpu.VMEM((4, ncp, rows + 2 * halo, LANES), F32),
            pltpu.VMEM((ncp, nrt + 2, 4, ROWS8, LANES), F32),
            pltpu.VMEM((ncp, nrt + 2, 4, ROWS8, LANES), F32),
            pltpu.VMEM((ncp, nrt + 2, ROWS8, LANES), F32),
            pltpu.VMEM((ncp, nrt + 2, ROWS8, LANES), F32),
            pltpu.VMEM((ncp, nrt, 5, ROWS8, LANES), F32),
            pltpu.VMEM((ncp, nrt, ROWS8, LANES), F32),
            pltpu.VMEM((ncp, nrt, ROWS8, LANES), F32),
            pltpu.VMEM((ncp * nrt * ROWS8, LANES), F32),
            pltpu.VMEM(((rows + 2 * halo) * ntr * inner, LANES), F32),
            pltpu.SemaphoreType.DMA((3,)),
        ],
        name="window",
    )(tile, south, north, ocean, ocean_south, ocean_north, interaction)


def shift(array, axis, by):
    count = lax.axis_size(axis)
    if by > 0:
        return lax.ppermute(array, axis, [(i, i + 1) for i in range(count - 1)])
    return lax.ppermute(array, axis, [(i + 1, i) for i in range(count - 1)])


def shards(ocean_fields, tracers, wet_levels, interaction):
    tiles = lax.axis_size("gx")
    ntr = tracers.shape[0]
    rows = ocean_fields.shape[1]
    columns = wet_levels.shape[1]
    levels = tracers.shape[2] // columns
    lines = tracers.shape[2] // LANES
    pair = LANES // levels
    inner = lines // tiles
    edge = HALO // pair
    ncp = inner + 2 * edge
    planes = ntr + 1

    margin = edge * LANES
    from_west = shift(ocean_fields[:, :, -margin:], "gx", 1)
    from_east = shift(ocean_fields[:, :, :margin], "gx", -1)
    depth = jnp.broadcast_to(wet_levels.astype(F32).reshape(lines, pair, 1), (lines, pair, levels))
    sent = cut_windows(tracers.reshape(ntr, lines, 1, LANES), depth.reshape(1, lines, 1, LANES), tiles, ncp)
    ocean = jnp.concatenate([from_west, ocean_fields, from_east], axis=2)
    ocean_south = shift(ocean[:, -HALO:], "grp", 1)
    ocean_north = shift(ocean[:, :HALO], "grp", -1)
    sent, ocean, ocean_south, ocean_north = lax.optimization_barrier((sent, ocean, ocean_south, ocean_north))
    tile = lax.all_to_all(sent.reshape(tiles, planes * ncp, LANES), "gx", split_axis=0, concat_axis=0, tiled=True)
    south = shift(tile[-HALO:], "grp", 1)
    north = shift(tile[:HALO], "grp", -1)
    ocean_next, result = run_window(
        tile.reshape(-1, LANES), south.reshape(-1, LANES), north.reshape(-1, LANES),
        ocean, ocean_south, ocean_north, interaction, ntr, ncp,
    )
    back = lax.all_to_all(result.reshape(tiles, ntr * inner, LANES), "gx", split_axis=0, concat_axis=0, tiled=True)
    back = back.reshape(tiles, ntr, inner, LANES).transpose(1, 0, 2, 3)
    return ocean_next, back.reshape(ntr, 1, lines * LANES)


def solution(mesh):
    placed = (P(None, "grp", "gx"), P(None, ("grp", "gx"), None), P(("grp", "gx"), None), P())
    return jax.shard_map(
        shards,
        mesh=mesh,
        in_specs=placed,
        out_specs=(P(None, "grp", "gx"), P(None, ("grp", "gx"), None)),
        check_vma=False,
    )
```

time: 270 us -> 172 us (0.64)
  Pallas kernels: 137 us -> 39.8 us
    pallas_call x1, Pallas kernels: 133 us -> 36 us  [run_window(): pl.pallas_call(main_kernel, out_shape=(jax.ShapeDtypeStruct((4, rows, inn...]
  transfers between devices with their start and end apart: 6 -> 6, of which waited for: 4 -> 4; matrix products, arithmetic and copies ran while one was open for 1% -> 1% of each run, Pallas kernels for 1% -> 2%
where the time goes in v2:
time: 172 us
  blocking collectives  96.5 us (56%)
  Pallas kernels  39.8 us (23%)
  starting transfers between devices  18 us (10%)
  waiting for transfers between devices  9.07 us (5%)
  local copies, waits for them, and re-layouts  7.55 us (4%)
    all_to_all x1, blocking collectives, shards(): lax.all_to_all(sent.reshape(tiles, planes * ncp, LANES), 'gx', split_axis...  61 us
    pallas_call x1, Pallas kernels, run_window(): pl.pallas_call(main_kernel, out_shape=(jax.ShapeDtypeStruct((4, rows, inn...  36 us
    all_to_all x1, blocking collectives, shards(): lax.all_to_all(result.reshape(tiles, ntr * inner, LANES), 'gx', split_axi...  35.4 us
    ppermute x3, starting transfers between devices, shift(): return lax.ppermute(array, axis, [(i + 1, i) for i in range(count - 1)])  9 us
    ppermute x3, starting transfers between devices, shift(): return lax.ppermute(array, axis, [(i, i + 1) for i in range(count - 1)])  8.96 us
    ppermute x3, waiting for transfers between devices, shift(): return lax.ppermute(array, axis, [(i + 1, i) for i in range(count - 1)])  6.97 us
    pallas_call x1, Pallas kernels, cut_windows(): pl.pallas_call(window_kernel, out_shape=jax.ShapeDtypeStruct((tiles, plan...  3.86 us
    unnamed x16, local copies, waits for them, and re-layouts  3.74 us
  transfers between devices with their start and end apart: 6, of which 4 were waited for; matrix products, arithmetic and copies ran while one was open for 1% of the time, Pallas kernels for 2%

profile of v2, /device:TPU:1, one launch (start us, length us, event | category | flops | bytes accessed | tf_op | source)
XLA Modules:
  0.0 171.7 jit_solution(10912814642628060945)
XLA Ops:
  0.6 0.0 copy-start.6
  0.6 1.0 fusion.2
  1.6 3.9 %collective-permute-start = (f32[4,32,256]{2,1,0:T(8,128)S(1)}, f32[4,32,256]{2,1,0:T(8,128)S(1)}, u32[]{:S(2)}, u32[]{:S(2)}) collective-permute-start(f32[4,32,256]{2,1,0:T(8,128)S(1)} %get-tuple-element.19), channel_id=1, source_target_pairs={{0,1},{1,2},{2,3},{3,4},{4,5},{5,6},{6,7},{7,8},{8,9},{9,10},{10,1... | collective-permute-start | bytes 393224 | tf_op jit(solution)/shard_map/ppermute | solution.py:355
  5.6 1.3 collective-permute-start.1
  6.9 0.9 collective-permute-done
  7.8 1.1 constant_dynamic-update-slice_fusion.1
  8.8 2.5 %collective-permute-done.1 = f32[4,32,256]{2,1,0:T(8,128)S(1)} collective-permute-done((f32[4,32,256]{2,1,0:T(8,128)S(1)}, f32[4,32,256]{2,1,0:T(8,128)S(1)}, u32[]{:S(2)}, u32[]{:S(2)}) %collective-permute-start.1) | collective-permute-done | bytes 131104 | tf_op jit(solution)/shard_map/ppermute | solution.py:356
  11.3 0.0 copy-start.1
  11.4 4.0 %collective-permute-start.3 = (f32[4,4,1536]{2,1,0:T(4,128)S(1)}, f32[4,4,1536]{2,1,0:T(4,128)S(1)}, u32[]{:S(2)}, u32[]{:S(2)}) collective-permute-start(f32[4,4,1536]{2,1,0:T(4,128)S(1)} %get-tuple-element.16), channel_id=1, source_target_pairs={{32,0},{64,32},{96,64},{33,1},{65,33},{97,65},{34,2},{66,34},{98,6... | collective-permute-start | bytes 294920 | tf_op jit(solution)/shard_map/ppermute | solution.py:356
  15.4 3.1 %collective-permute-start.2 = (f32[4,4,1536]{2,1,0:T(4,128)S(1)}, f32[4,4,1536]{2,1,0:T(4,128)S(1)}, u32[]{:S(2)}, u32[]{:S(2)}) collective-permute-start(f32[4,4,1536]{2,1,0:T(4,128)S(1)} %get-tuple-element.17), channel_id=1, source_target_pairs={{0,32},{32,64},{64,96},{1,33},{33,65},{65,97},{2,34},{34,66},{66,9... | collective-permute-start | bytes 294920 | tf_op jit(solution)/shard_map/ppermute | solution.py:355
  18.5 0.0 copy-done.6
  18.5 0.1 broadcast_in_dim.7
  18.7 0.1 copy.7
  18.8 0.8 copy.8.depth_plane
  19.5 3.9 %cut_windows.1 = f32[32,20,12,1,128]{4,3,2,1,0:T(1,128)} custom-call(f32[19,256,1,128]{3,2,1,0:T(1,128)} %bitcast.14, f32[1,256,1,128]{3,2,1,0:T(1,128)} %copy.8.depth_plane), custom_call_target="tpu_custom_call" | custom-call | tf_op jit(solution)/shard_map/cut_windows/pallas_call | solution.py:67
  23.4 0.0 copy-done.1
  23.4 0.0 collective-permute-done.3.ocean_north
  23.4 0.0 copy-start.4
  23.4 0.0 collective-permute-done.2.ocean_south
  23.4 0.0 copy-start.5
  23.4 61.0 %all_to_all.10 = f32[32,240,128]{2,1,0:T(8,128)S(1)} all-to-all(f32[32,240,128]{2,1,0:T(8,128)} %bitcast.12), channel_id=1, replica_groups=mesh['grp'=4,'gx'=32] {'gx'}, dimensions={0} | all-to-all | bytes 7864320 | tf_op jit(solution)/shard_map/all_to_all | solution.py:381
  84.5 0.0 copy-done.4
  84.5 0.0 copy-done.5
  84.5 0.0 copy-start
  84.5 1.9 %copy-done = f32[32,240,128]{2,1,0:T(8,128)} copy-done((f32[32,240,128]{2,1,0:T(8,128)}, f32[32,240,128]{2,1,0:T(8,128)S(1)}, u32[]{:S(2)}) %copy-start) | copy-done | bytes 3932184
  86.3 0.1 fusion
  86.4 3.7 %collective-permute-start.5 = (f32[4,240,128]{2,1,0:T(8,128)S(1)}, f32[4,240,128]{2,1,0:T(8,128)S(1)}, u32[]{:S(2)}, u32[]{:S(2)}) collective-permute-start(f32[4,240,128]{2,1,0:T(8,128)S(1)} %get-tuple-element.14), channel_id=1, source_target_pairs={{32,0},{64,32},{96,64},{33,1},{65,33},{97,65},{34,2},{66,34},{98,6... | collective-permute-start | bytes 1474568 | tf_op jit(solution)/shard_map/ppermute | solution.py:356
  90.1 1.9 %collective-permute-start.4 = (f32[4,240,128]{2,1,0:T(8,128)S(1)}, f32[4,240,128]{2,1,0:T(8,128)S(1)}, u32[]{:S(2)}, u32[]{:S(2)}) collective-permute-start(f32[4,240,128]{2,1,0:T(8,128)S(1)} %get-tuple-element.15), channel_id=1, source_target_pairs={{0,32},{32,64},{64,96},{1,33},{33,65},{65,97},{2,34},{34,66},{66,9... | collective-permute-start | bytes 1474568 | tf_op jit(solution)/shard_map/ppermute | solution.py:355
  92.0 4.5 %collective-permute-done.5 = f32[4,240,128]{2,1,0:T(8,128)S(1)} collective-permute-done((f32[4,240,128]{2,1,0:T(8,128)S(1)}, f32[4,240,128]{2,1,0:T(8,128)S(1)}, u32[]{:S(2)}, u32[]{:S(2)}) %collective-permute-start.5) | collective-permute-done | bytes 491552 | tf_op jit(solution)/shard_map/ppermute | solution.py:356
  96.6 0.0 copy-start.2
  96.6 1.2 collective-permute-done.4
  97.8 0.0 copy-start.3
  97.8 0.0 copy-done.2
  97.8 0.8 copy-done.3
  98.6 36.0 %window.1 = (f32[4,32,1024]{2,1,0:T(8,128)}, f32[4864,128]{1,0:T(8,128)}) custom-call(f32[7680,128]{1,0:T(8,128)} %bitcast.11, f32[960,128]{1,0:T(8,128)} %bitcast.19, f32[960,128]{1,0:T(8,128)} %bitcast.18, f32[4,32,1536]{2,1,0:T(8,128)} %copy-done.1, f32[4,4,1536]{2,1,0:T(4,128)} %copy-done.5, f32[4,4,1536]{2,1,0:T(4,128)} %copy-done.4, f32[19,19]{1,0:T(8,128)} %mix_ref.1), custom_call_target="tpu_custom_call" | custom-call | tf_op jit(solution)/shard_map/window/pallas_call | solution.py:324
  134.6 35.4 %all_to_all.11 = f32[32,152,128]{2,1,0:T(8,128)S(1)} all-to-all(f32[32,152,128]{2,1,0:T(8,128)} %bitcast.15), channel_id=1, replica_groups=mesh['grp'=4,'gx'=32] {'gx'}, dimensions={0} | all-to-all | bytes 4980736 | tf_op jit(solution)/shard_map/all_to_all | solution.py:388
  170.0 1.7 %copy.9 = f32[32,19,8,128]{3,2,0,1:T(8,128)} copy(f32[32,19,8,128]{3,2,1,0:T(8,128)S(1)} %bitcast.13) | data formatting | bytes 4980736 | tf_op jit(solution)/shard_map/reshape | solution.py:389
  (5 shorter events, 0.1 us)
Async XLA Ops:
  0.6 17.9 %copy-start.6 = (s32[1,512]{1,0:T(1,128)S(1)}, s32[1,512]{1,0:T(1,128)}, u32[]{:S(2)}) copy-start(s32[1,512]{1,0:T(1,128)} %param.6) | copy-start | bytes 6148
  1.6 6.1 %collective-permute-start = (f32[4,32,256]{2,1,0:T(8,128)S(1)}, f32[4,32,256]{2,1,0:T(8,128)S(1)}, u32[]{:S(2)}, u32[]{:S(2)}) collective-permute-start(f32[4,32,256]{2,1,0:T(8,128)S(1)} %get-tuple-element.19), channel_id=1, source_target_pairs={{0,1},{1,2},{2,3},{3,4},{4,5},{5,6},{6,7},{7,8},{8,9},{9,10},{10,1... | collective-permute-start | bytes 393224 | tf_op jit(solution)/shard_map/ppermute | solution.py:355
  5.6 5.7 %collective-permute-start.1 = (f32[4,32,256]{2,1,0:T(8,128)S(1)}, f32[4,32,256]{2,1,0:T(8,128)S(1)}, u32[]{:S(2)}, u32[]{:S(2)}) collective-permute-start(f32[4,32,256]{2,1,0:T(8,128)S(1)} %get-tuple-element.18), channel_id=1, source_target_pairs={{1,0},{2,1},{3,2},{4,3},{5,4},{6,5},{7,6},{8,7},{9,8},{10,9},{11,1... | collective-permute-start | bytes 393224 | tf_op jit(solution)/shard_map/ppermute | solution.py:356
  11.3 12.1 %copy-start.1 = (f32[4,32,1536]{2,1,0:T(8,128)}, f32[4,32,1536]{2,1,0:T(8,128)S(1)}, u32[]{:S(2)}) copy-start(f32[4,32,1536]{2,1,0:T(8,128)S(1)} %constant_dynamic-update-slice_fusion.ocean) | copy-start | bytes 2359300
  11.4 12.0 %collective-permute-start.3 = (f32[4,4,1536]{2,1,0:T(4,128)S(1)}, f32[4,4,1536]{2,1,0:T(4,128)S(1)}, u32[]{:S(2)}, u32[]{:S(2)}) collective-permute-start(f32[4,4,1536]{2,1,0:T(4,128)S(1)} %get-tuple-element.16), channel_id=1, source_target_pairs={{32,0},{64,32},{96,64},{33,1},{65,33},{97,65},{34,2},{66,34},{98,6... | collective-permute-start | bytes 294920 | tf_op jit(solution)/shard_map/ppermute | solution.py:356
  15.4 8.0 %collective-permute-start.2 = (f32[4,4,1536]{2,1,0:T(4,128)S(1)}, f32[4,4,1536]{2,1,0:T(4,128)S(1)}, u32[]{:S(2)}, u32[]{:S(2)}) collective-permute-start(f32[4,4,1536]{2,1,0:T(4,128)S(1)} %get-tuple-element.17), channel_id=1, source_target_pairs={{0,32},{32,64},{64,96},{1,33},{33,65},{65,97},{2,34},{34,66},{66,9... | collective-permute-start | bytes 294920 | tf_op jit(solution)/shard_map/ppermute | solution.py:355
  23.4 61.1 %copy-start.4 = (f32[4,4,1536]{2,1,0:T(4,128)}, f32[4,4,1536]{2,1,0:T(4,128)S(1)}, u32[]{:S(2)}) copy-start(f32[4,4,1536]{2,1,0:T(4,128)S(1)} %collective-permute-done.3.ocean_north) | copy-start | bytes 294916
  23.4 61.1 %copy-start.5 = (f32[4,4,1536]{2,1,0:T(4,128)}, f32[4,4,1536]{2,1,0:T(4,128)S(1)}, u32[]{:S(2)}) copy-start(f32[4,4,1536]{2,1,0:T(4,128)S(1)} %collective-permute-done.2.ocean_south) | copy-start | bytes 294916
  84.5 1.9 %copy-start = (f32[32,240,128]{2,1,0:T(8,128)}, f32[32,240,128]{2,1,0:T(8,128)S(1)}, u32[]{:S(2)}) copy-start(f32[32,240,128]{2,1,0:T(8,128)S(1)} %all_to_all.10) | copy-start | bytes 11796484
  86.4 10.1 %collective-permute-start.5 = (f32[4,240,128]{2,1,0:T(8,128)S(1)}, f32[4,240,128]{2,1,0:T(8,128)S(1)}, u32[]{:S(2)}, u32[]{:S(2)}) collective-permute-start(f32[4,240,128]{2,1,0:T(8,128)S(1)} %get-tuple-element.14), channel_id=1, source_target_pairs={{32,0},{64,32},{96,64},{33,1},{65,33},{97,65},{34,2},{66,34},{98,6... | collective-permute-start | bytes 1474568 | tf_op jit(solution)/shard_map/ppermute | solution.py:356
  90.1 7.7 %collective-permute-start.4 = (f32[4,240,128]{2,1,0:T(8,128)S(1)}, f32[4,240,128]{2,1,0:T(8,128)S(1)}, u32[]{:S(2)}, u32[]{:S(2)}) collective-permute-start(f32[4,240,128]{2,1,0:T(8,128)S(1)} %get-tuple-element.15), channel_id=1, source_target_pairs={{0,32},{32,64},{64,96},{1,33},{33,65},{65,97},{2,34},{34,66},{66,9... | collective-permute-start | bytes 1474568 | tf_op jit(solution)/shard_map/ppermute | solution.py:355
  96.6 1.2 copy-start.2
  97.8 0.8 copy-start.3

commit v3 on v2

--- a/solution.py
+++ b/solution.py
@@ -68,19 +68,77 @@
         window_kernel,
         out_shape=jax.ShapeDtypeStruct((tiles, planes, wide, 1, LANES), F32),
         in_specs=[anywhere, anywhere],
-        out_specs=anywhere,
+        out_specs=pl.BlockSpec(memory_space=pltpu.HBM),
         scratch_shapes=[
             pltpu.VMEM((planes, lines + 2 * edge, 1, LANES), F32),
             pltpu.SemaphoreType.DMA((2,)),
             pltpu.SemaphoreType.DMA((tiles,)),
         ],
+        compiler_params=pltpu.CompilerParams(vmem_limit_bytes=16 * 2**20),
         name="cut_windows",
     )(strip, depth_plane)
 
 
+def edge_kernel(tile, west, ocean, east, to_north, to_south, lines, sem):
+    planes_lines = tile.shape[1]
+    rows = ocean.shape[1]
+    halo = HALO
+    wide = lines.shape[1] // halo
+    sides = ((to_north, rows - halo), (to_south, 0))
+    copies = [
+        pltpu.make_async_copy(
+            tile.at[first + r],
+            message.at[pl.ds(r * (planes_lines + wide), planes_lines)],
+            sem.at[k * halo + r],
+        )
+        for k, (message, first) in enumerate(sides)
+        for r in range(halo)
+    ]
+    for copy in copies:
+        copy.start()
+    for k, (message, first) in enumerate(sides):
+        c = 0
+        for f in range(4):
+            for part in (west, ocean, east):
+                for j in range(part.shape[2] // LANES):
+                    lines[k, pl.ds(c, halo, stride=wide), :] = part[f, pl.ds(first, halo), pl.ds(j * LANES, LANES)]
+                    c += 1
+    more = [
+        pltpu.make_async_copy(
+            lines.at[k, pl.ds(r * wide, wide)],
+            message.at[pl.ds(r * (planes_lines + wide) + planes_lines, wide)],
+            sem.at[(2 + k) * halo + r],
+        )
+        for k, (message, first) in enumerate(sides)
+        for r in range(halo)
+    ]
+    for copy in more:
+        copy.start()
+    for copy in copies + more:
+        copy.wait()
+
+
+def row_messages(tile, west, ocean, east, ncp):
+    anywhere = pl.BlockSpec(memory_space=pl.ANY)
+    inside = pl.BlockSpec(memory_space=pltpu.VMEM)
+    message = jax.ShapeDtypeStruct((HALO * (tile.shape[1] + 4 * ncp), LANES), F32)
+    return pl.pallas_call(
+        edge_kernel,
+        out_shape=(message, message),
+        in_specs=[anywhere, inside, inside, inside],
+        out_specs=(anywhere, anywhere),
+        scratch_shapes=[
+            pltpu.VMEM((2, HALO * 4 * ncp, LANES), F32),
+            pltpu.SemaphoreType.DMA((4 * HALO,)),
+        ],
+        compiler_params=pltpu.CompilerParams(vmem_limit_bytes=8 * 2**20),
+        name="row_messages",
+    )(tile, west, ocean, east)
+
+
 def main_kernel(
-    tile, south, north, ocean, ocean_south, ocean_north, mix_ref, ocean_out, out,
-    raw, stock_a, stock_b, sea, ocean_a, ocean_b, press, wet, weights, growth0, growth, flat, result, sem,
+    tile, south, north, west, ocean, east, mix_ref, ocean_out, out,
+    raw, stock_a, stock_b, sea, beyond, ocean_a, ocean_b, press, wet, weights, growth0, growth, flat, result, sem,
 ):
     ncp, nrt, ntr = stock_a.shape[0], stock_a.shape[1] - 2, stock_a.shape[2]
     planes = ntr + 1
@@ -88,11 +146,22 @@
     rows = tile.shape[0] // line_stride
     halo = HALO
     inner = ncp - halo
+    wide_ocean = 4 * ncp
     copies = [
-        pltpu.make_async_copy(south, raw.at[pl.ds(0, halo * line_stride)], sem.at[0]),
-        pltpu.make_async_copy(tile, raw.at[pl.ds(halo * line_stride, rows * line_stride)], sem.at[1]),
-        pltpu.make_async_copy(north, raw.at[pl.ds((halo + rows) * line_stride, halo * line_stride)], sem.at[2]),
+        pltpu.make_async_copy(tile, raw.at[pl.ds(halo * line_stride, rows * line_stride)], sem.at[0]),
     ]
+    for side, message in enumerate((south, north)):
+        for r in range(halo):
+            start = r * (line_stride + wide_ocean)
+            row = r + side * (halo + rows)
+            copies.append(pltpu.make_async_copy(
+                message.at[pl.ds(start, line_stride)], raw.at[pl.ds(row * line_stride, line_stride)],
+                sem.at[len(copies)],
+            ))
+            copies.append(pltpu.make_async_copy(
+                message.at[pl.ds(start + line_stride, wide_ocean)], beyond.at[side, pl.ds(r * wide_ocean, wide_ocean)],
+                sem.at[len(copies)],
+            ))
     for copy in copies:
         copy.start()
 
@@ -138,30 +207,38 @@
             + jnp.dot(low, upper, preferred_element_type=F32)
         )
 
+    wide = ntr * ROWS8
+    deep = (ntr + 1) * ROWS8
+    pick = (lax.broadcasted_iota(jnp.int32, (wide, ntr), 0) // ROWS8 == lax.broadcasted_iota(jnp.int32, (wide, ntr), 1)).astype(F32).astype(BF16)
+    pick_t = (lax.broadcasted_iota(jnp.int32, (ntr, deep), 1) // ROWS8 == lax.broadcasted_iota(jnp.int32, (ntr, deep), 0)).astype(F32).astype(BF16)
+    same = lax.broadcasted_iota(jnp.int32, (wide, deep), 0) % ROWS8 == lax.broadcasted_iota(jnp.int32, (wide, deep), 1) % ROWS8
+
+    def spread(part):
+        tall = jnp.dot(pick, part, preferred_element_type=F32).astype(BF16)
+        return jnp.where(same, jnp.dot(tall, pick_t, preferred_element_type=F32), 0.0)
+
+    mix = mix_ref[...]
+    mix_hi = mix.astype(BF16)
+    mix_lo = (mix - mix_hi.astype(F32)).astype(BF16)
+    spread_hi = spread(mix_hi)
+    mix_all = jnp.concatenate([spread_hi, spread_hi, spread(mix_lo)], axis=1).astype(BF16)
+
+    for copy in copies:
+        copy.wait()
+
     for f in range(4):
         for cp in range(ncp):
-            across = pl.ds(cp * LANES, LANES)
-            sea[f, cp, pl.ds(0, halo), :] = ocean_south[f, :, across]
-            sea[f, cp, pl.ds(halo, rows), :] = ocean[f, :, across]
-            sea[f, cp, pl.ds(halo + rows, halo), :] = ocean_north[f, :, across]
+            if cp < halo // 2:
+                part, j = west, cp
+            elif cp < ncp - halo // 2:
+                part, j = ocean, cp - halo // 2
+            else:
+                part, j = east, cp - (ncp - halo // 2)
+            sea[f, cp, pl.ds(0, halo), :] = beyond[0, pl.ds(f * ncp + cp, halo, stride=wide_ocean), :]
+            sea[f, cp, pl.ds(halo, rows), :] = part[f, :, pl.ds(j * LANES, LANES)]
+            sea[f, cp, pl.ds(halo + rows, halo), :] = beyond[1, pl.ds(f * ncp + cp, halo, stride=wide_ocean), :]
             for q in range(nrt):
                 put(ocean_a, cp, q, sea[f, cp, pl.ds(q, ROWS8, stride=nrt), :], f)
-
-    wide = ntr * ROWS8
-    pick = (lax.broadcasted_iota(jnp.int32, (wide, ntr), 0) // ROWS8 == lax.broadcasted_iota(jnp.int32, (wide, ntr), 1)).astype(F32)
-    deep = (ntr + 1) * ROWS8
-    pick_t = (lax.broadcasted_iota(jnp.int32, (ntr, deep), 1) // ROWS8 == lax.broadcasted_iota(jnp.int32, (ntr, deep), 0)).astype(F32)
-    spread = jnp.dot(
-        jnp.dot(pick, mix_ref[...], precision=lax.Precision.HIGHEST, preferred_element_type=F32),
-        pick_t, precision=lax.Precision.HIGHEST, preferred_element_type=F32,
-    )
-    same = lax.broadcasted_iota(jnp.int32, (wide, deep), 0) % ROWS8 == lax.broadcasted_iota(jnp.int32, (wide, deep), 1) % ROWS8
-    spread = jnp.where(same, spread, 0.0)
-    mix_hi = spread.astype(BF16).astype(F32)
-    mix_all = jnp.concatenate([mix_hi, mix_hi, spread - mix_hi], axis=1).astype(BF16)
-
-    for copy in copies:
-        copy.wait()
 
     @pl.loop(0, ncp)
     def _(cp):
@@ -261,16 +338,14 @@
         def _(cp):
             def begin(q):
                 weight = [weights[cp, q, k] for k in range(5)]
-                advected, high, low = [], [], []
+                advected, parts = [], []
                 for t in range(ntr):
                     a = carry(old, cp, q, t, weight)
-                    s = a / (saturation + jnp.abs(a))
-                    h = s.astype(BF16).astype(F32)
                     advected.append(a)
-                    high.append(h)
-                    low.append(s - h)
-                high = jnp.concatenate(high + [blank], axis=0).astype(BF16)
-                low = jnp.concatenate(low + [blank], axis=0).astype(BF16)
+                    parts.append(a / (saturation + jnp.abs(a)))
+                s = jnp.concatenate(parts + [blank], axis=0)
+                high = s.astype(BF16)
+                low = (s - high.astype(F32)).astype(BF16)
                 return advected, jnp.concatenate([high, low, high], axis=0)
 
             def end(group, begun):
@@ -314,7 +389,7 @@
     send.wait()
 
 
-def run_window(tile, south, north, ocean, ocean_south, ocean_north, interaction, ntr, ncp):
+def run_window(tile, south, north, west, ocean, east, interaction, ntr, ncp):
     rows = ocean.shape[1]
     halo = HALO
     nrt = (rows + 2 * halo) // ROWS8
@@ -334,6 +409,7 @@
             pltpu.VMEM((ncp, nrt + 2, ntr, ROWS8, LANES), F32),
             pltpu.VMEM((ncp, nrt + 2, ntr, ROWS8, LANES), F32),
             pltpu.VMEM((4, ncp, rows + 2 * halo, LANES), F32),
+            pltpu.VMEM((2, halo * 4 * ncp, LANES), F32),
             pltpu.VMEM((ncp, nrt + 2, 4, ROWS8, LANES), F32),
             pltpu.VMEM((ncp, nrt + 2, 4, ROWS8, LANES), F32),
             pltpu.VMEM((ncp, nrt + 2, ROWS8, LANES), F32),
@@ -343,10 +419,11 @@
             pltpu.VMEM((ncp, nrt, ROWS8, LANES), F32),
             pltpu.VMEM((ncp * nrt * ROWS8, LANES), F32),
             pltpu.VMEM(((rows + 2 * halo) * ntr * inner, LANES), F32),
-            pltpu.SemaphoreType.DMA((3,)),
+            pltpu.SemaphoreType.DMA((1 + 4 * halo,)),
         ],
+        compiler_params=pltpu.CompilerParams(vmem_limit_bytes=40 * 2**20),
         name="window",
-    )(tile, south, north, ocean, ocean_south, ocean_north, interaction)
+    )(tile, south, north, west, ocean, east, interaction)
 
 
 def shift(array, axis, by):
@@ -374,16 +451,12 @@
     from_east = shift(ocean_fields[:, :, :margin], "gx", -1)
     depth = jnp.broadcast_to(wet_levels.astype(F32).reshape(lines, pair, 1), (lines, pair, levels))
     sent = cut_windows(tracers.reshape(ntr, lines, 1, LANES), depth.reshape(1, lines, 1, LANES), tiles, ncp)
-    ocean = jnp.concatenate([from_west, ocean_fields, from_east], axis=2)
-    ocean_south = shift(ocean[:, -HALO:], "grp", 1)
-    ocean_north = shift(ocean[:, :HALO], "grp", -1)
-    sent, ocean, ocean_south, ocean_north = lax.optimization_barrier((sent, ocean, ocean_south, ocean_north))
     tile = lax.all_to_all(sent.reshape(tiles, planes * ncp, LANES), "gx", split_axis=0, concat_axis=0, tiled=True)
-    south = shift(tile[-HALO:], "grp", 1)
-    north = shift(tile[:HALO], "grp", -1)
+    to_north, to_south = row_messages(tile, from_west, ocean_fields, from_east, ncp)
+    south = shift(to_north, "grp", 1)
+    north = shift(to_south, "grp", -1)
     ocean_next, result = run_window(
-        tile.reshape(-1, LANES), south.reshape(-1, LANES), north.reshape(-1, LANES),
-        ocean, ocean_south, ocean_north, interaction, ntr, ncp,
+        tile.reshape(-1, LANES), south, north, from_west, ocean_fields, from_east, interaction, ntr, ncp
     )
     back = lax.all_to_all(result.reshape(tiles, ntr * inner, LANES), "gx", split_axis=0, concat_axis=0, tiled=True)
     back = back.reshape(tiles, ntr, inner, LANES).transpose(1, 0, 2, 3)

time: 172 us -> 158 us (0.919)
  blocking collectives: 96.5 us -> 34.8 us
  waiting for transfers between devices: 9.07 us -> 53.1 us
  starting transfers between devices: 18 us -> 24.9 us
  Pallas kernels: 39.8 us -> 37.3 us
  local copies, waits for them, and re-layouts: 7.55 us -> 5.65 us
    all_to_all x1 -> x0, blocking collectives: 61 us -> none  [shards(): lax.all_to_all(sent.reshape(tiles, planes * ncp, LANES), 'gx', split_axis...]
    ppermute x3 -> x2, waiting for transfers between devices: 6.97 us -> 47.2 us  [shift(): return lax.ppermute(array, axis, [(i + 1, i) for i in range(count - 1)])]
    all_to_all x0 -> x1, starting transfers between devices: none -> 11.6 us  [shards(): lax.all_to_all(sent.reshape(tiles, planes * ncp, LANES), 'gx', split_axis...]
    ppermute x3 -> x2, starting transfers between devices: 9 us -> 3.21 us  [shift(): return lax.ppermute(array, axis, [(i + 1, i) for i in range(count - 1)])]
    ppermute x3 -> x2, waiting for transfers between devices: 2.1 us -> 4.88 us  [shift(): return lax.ppermute(array, axis, [(i, i + 1) for i in range(count - 1)])]
    pallas_call x1, Pallas kernels: 3.86 us -> 1.53 us  [cut_windows(): pl.pallas_call(window_kernel, out_shape=jax.ShapeDtypeStruct((tiles, plan...]
    ppermute x3 -> x2, starting transfers between devices: 8.96 us -> 10.1 us  [shift(): return lax.ppermute(array, axis, [(i, i + 1) for i in range(count - 1)])]
    unnamed x16 -> x8, local copies, waits for them, and re-layouts: 3.74 us -> 3.59 us
  transfers between devices with their start and end apart: 6 -> 5, of which waited for: 4 -> 4; matrix products, arithmetic and copies ran while one was open for 1% -> 0% of each run, Pallas kernels for 2% -> 0%
where the time goes in v3:
time: 158 us; the launch traced here: 157 us
  waiting for transfers between devices  53.1 us (34%)
  Pallas kernels  37.3 us (24%)
  blocking collectives  34.8 us (22%)
  starting transfers between devices  24.9 us (16%)
  local copies, waits for them, and re-layouts  5.65 us (4%)
    ppermute x2, waiting for transfers between devices, shift(): return lax.ppermute(array, axis, [(i + 1, i) for i in range(count - 1)])  47.2 us
    all_to_all x1, blocking collectives, shards(): lax.all_to_all(result.reshape(tiles, ntr * inner, LANES), 'gx', split_axi...  34.8 us
    pallas_call x1, Pallas kernels, run_window(): pl.pallas_call(main_kernel, out_shape=(jax.ShapeDtypeStruct((4, rows, inn...  34.3 us
    all_to_all x1, starting transfers between devices, shards(): lax.all_to_all(sent.reshape(tiles, planes * ncp, LANES), 'gx', split_axis...  11.6 us
    ppermute x2, starting transfers between devices, shift(): return lax.ppermute(array, axis, [(i, i + 1) for i in range(count - 1)])  10.1 us
    ppermute x2, waiting for transfers between devices, shift(): return lax.ppermute(array, axis, [(i, i + 1) for i in range(count - 1)])  4.88 us
    unnamed x8, local copies, waits for them, and re-layouts  3.59 us
    ppermute x2, starting transfers between devices, shift(): return lax.ppermute(array, axis, [(i + 1, i) for i in range(count - 1)])  3.21 us
  transfers between devices with their start and end apart: 5, of which 4 were waited for; matrix products, arithmetic and copies ran while one was open for 0% of the time, Pallas kernels for 0%

profile of v3, /device:TPU:1, one launch (start us, length us, event | category | flops | bytes accessed | tf_op | source)
XLA Modules:
  0.0 157.1 jit_solution(8646927361905809000)
XLA Ops:
  0.6 0.7 convert_reduce_fusion
  1.3 0.1 broadcast_in_dim.7
  1.5 0.1 copy.7
  1.6 0.1 copy.8.depth_plane
  1.7 0.0 copy-start.2
  1.7 1.7 %copy-done.2 = f32[19,1,32768]{2,1,0:T(1,128)S(1)} copy-done((f32[19,1,32768]{2,1,0:T(1,128)S(1)}, f32[19,1,32768]{2,1,0:T(1,128)}, u32[]{:S(2)}) %copy-start.2) | copy-done | bytes 2490392
  3.4 1.5 cut_windows.1
  4.9 0.0 copy-start
  4.9 1.9 %copy-done = f32[32,20,12,1,128]{4,3,2,1,0:T(1,128)} copy-done((f32[32,20,12,1,128]{4,3,2,1,0:T(1,128)}, f32[32,20,12,1,128]{4,3,2,1,0:T(1,128)S(1)}, u32[]{:S(2)}) %copy-start) | copy-done | bytes 3932184
  6.8 0.0 copy-start.1
  6.8 11.6 %all-to-all-start = ((f32[32,240,128]{2,1,0:T(8,128)}), f32[32,240,128]{2,1,0:T(8,128)}, u32[]{:S(2)}, u32[]{:S(2)}) async-start(f32[32,240,128]{2,1,0:T(8,128)} %bitcast.9), calls=%async_computation | async-start | bytes 7864320 | tf_op jit(solution)/shard_map/all_to_all | solution.py:454
  18.4 0.0 copy-done.1
  18.4 0.0 copy-start.3
  18.4 1.3 collective-permute-start.1
  19.7 4.0 %collective-permute-start = (f32[4,32,256]{2,1,0:T(8,128)S(1)}, f32[4,32,256]{2,1,0:T(8,128)S(1)}, u32[]{:S(2)}, u32[]{:S(2)}) collective-permute-start(f32[4,32,256]{2,1,0:T(8,128)S(1)} %get-tuple-element.11), channel_id=1, source_target_pairs={{0,1},{1,2},{2,3},{3,4},{4,5},{5,6},{6,7},{7,8},{8,9},{9,10},{10,1... | collective-permute-start | bytes 393224 | tf_op jit(solution)/shard_map/ppermute | solution.py:432
  23.7 42.9 %collective-permute-done.1.east = f32[4,32,256]{2,1,0:T(8,128)S(1)} collective-permute-done((f32[4,32,256]{2,1,0:T(8,128)S(1)}, f32[4,32,256]{2,1,0:T(8,128)S(1)}, u32[]{:S(2)}, u32[]{:S(2)}) %collective-permute-start.1) | collective-permute-done | bytes 131104 | tf_op jit(solution)/shard_map/ppermute | solution.py:433
  66.6 0.0 collective-permute-done.west
  66.6 1.0 all-to-all-done.tile
  67.6 1.4 row_messages.1
  69.0 6.1 %collective-permute-start.2 = (f32[1152,128]{1,0:T(8,128)S(1)}, f32[1152,128]{1,0:T(8,128)S(1)}, u32[]{:S(2)}, u32[]{:S(2)}) collective-permute-start(f32[1152,128]{1,0:T(8,128)S(1)} %get-tuple-element.6), channel_id=1, source_target_pairs={{0,32},{32,64},{64,96},{1,33},{33,65},{65,97},{2,34},{34,66},{66,9... | collective-permute-start | bytes 1769480 | tf_op jit(solution)/shard_map/ppermute | solution.py:432
  75.1 1.9 %collective-permute-start.3 = (f32[1152,128]{1,0:T(8,128)S(1)}, f32[1152,128]{1,0:T(8,128)S(1)}, u32[]{:S(2)}, u32[]{:S(2)}) collective-permute-start(f32[1152,128]{1,0:T(8,128)S(1)} %get-tuple-element.7), channel_id=1, source_target_pairs={{32,0},{64,32},{96,64},{33,1},{65,33},{97,65},{34,2},{66,34},{98,6... | collective-permute-start | bytes 1769480 | tf_op jit(solution)/shard_map/ppermute | solution.py:433
  77.0 4.9 %collective-permute-done.2.south = f32[1152,128]{1,0:T(8,128)S(1)} collective-permute-done((f32[1152,128]{1,0:T(8,128)S(1)}, f32[1152,128]{1,0:T(8,128)S(1)}, u32[]{:S(2)}, u32[]{:S(2)}) %collective-permute-start.2) | collective-permute-done | bytes 589856 | tf_op jit(solution)/shard_map/ppermute | solution.py:432
  81.9 4.4 %collective-permute-done.3.north = f32[1152,128]{1,0:T(8,128)S(1)} collective-permute-done((f32[1152,128]{1,0:T(8,128)S(1)}, f32[1152,128]{1,0:T(8,128)S(1)}, u32[]{:S(2)}, u32[]{:S(2)}) %collective-permute-start.3) | collective-permute-done | bytes 589856 | tf_op jit(solution)/shard_map/ppermute | solution.py:433
  86.3 0.0 copy-done.3
  86.3 34.3 %window.1 = (f32[4,32,1024]{2,1,0:T(8,128)}, f32[4864,128]{1,0:T(8,128)S(1)}) custom-call(f32[7680,128]{1,0:T(8,128)} %bitcast.3.tile, f32[1152,128]{1,0:T(8,128)S(1)} %collective-permute-done.2.south, f32[1152,128]{1,0:T(8,128)S(1)} %collective-permute-done.3.north, f32[4,32,256]{2,1,0:T(8,128)S(1)} %collective-permute-done.west, ...), custom_call_target="tpu_custom_call" | custom-call | tf_op jit(solution)/shard_map/window/pallas_call | solution.py:399
  120.6 34.8 %all_to_all.10 = f32[32,152,128]{2,1,0:T(8,128)S(1)} all-to-all(f32[32,152,128]{2,1,0:T(8,128)S(1)} %bitcast.11), channel_id=1, replica_groups=mesh['grp'=4,'gx'=32] {'gx'}, dimensions={0} | all-to-all | bytes 4980736 | tf_op jit(solution)/shard_map/all_to_all | solution.py:461
  155.4 1.7 %copy.9 = f32[32,19,8,128]{3,2,0,1:T(8,128)} copy(f32[32,19,8,128]{3,2,1,0:T(8,128)S(1)} %bitcast.12) | data formatting | bytes 4980736 | tf_op jit(solution)/shard_map/reshape | solution.py:462
  (2 shorter events, 0.0 us)
Async XLA Ops:
  1.7 1.7 %copy-start.2 = (f32[19,1,32768]{2,1,0:T(1,128)S(1)}, f32[19,1,32768]{2,1,0:T(1,128)}, u32[]{:S(2)}) copy-start(f32[19,1,32768]{2,1,0:T(1,128)} %param.5) | copy-start | bytes 7471108
  4.9 1.9 %copy-start = (f32[32,20,12,1,128]{4,3,2,1,0:T(1,128)}, f32[32,20,12,1,128]{4,3,2,1,0:T(1,128)S(1)}, u32[]{:S(2)}) copy-start(f32[32,20,12,1,128]{4,3,2,1,0:T(1,128)S(1)} %cut_windows.1) | copy-start | bytes 11796484
  6.8 11.6 %copy-start.1 = (f32[4,32,1024]{2,1,0:T(8,128)S(1)}, f32[4,32,1024]{2,1,0:T(8,128)}, u32[]{:S(2)}) copy-start(f32[4,32,1024]{2,1,0:T(8,128)} %ocean.3) | copy-start | bytes 1572868
  6.8 60.8 %all-to-all-start = ((f32[32,240,128]{2,1,0:T(8,128)}), f32[32,240,128]{2,1,0:T(8,128)}, u32[]{:S(2)}, u32[]{:S(2)}) async-start(f32[32,240,128]{2,1,0:T(8,128)} %bitcast.9), calls=%async_computation | async-start | bytes 7864320 | tf_op jit(solution)/shard_map/all_to_all | solution.py:454
  18.4 67.9 %copy-start.3 = (f32[19,19]{1,0:T(8,128)S(1)}, f32[19,19]{1,0:T(8,128)}, u32[]{:S(2)}) copy-start(f32[19,19]{1,0:T(8,128)} %mix_ref.1) | copy-start | bytes 4336
  18.4 48.2 %collective-permute-start.1 = (f32[4,32,256]{2,1,0:T(8,128)S(1)}, f32[4,32,256]{2,1,0:T(8,128)S(1)}, u32[]{:S(2)}, u32[]{:S(2)}) collective-permute-start(f32[4,32,256]{2,1,0:T(8,128)S(1)} %get-tuple-element.10), channel_id=1, source_target_pairs={{1,0},{2,1},{3,2},{4,3},{5,4},{6,5},{7,6},{8,7},{9,8},{10,9},{11,1... | collective-permute-start | bytes 393224 | tf_op jit(solution)/shard_map/ppermute | solution.py:433
  19.7 46.9 %collective-permute-start = (f32[4,32,256]{2,1,0:T(8,128)S(1)}, f32[4,32,256]{2,1,0:T(8,128)S(1)}, u32[]{:S(2)}, u32[]{:S(2)}) collective-permute-start(f32[4,32,256]{2,1,0:T(8,128)S(1)} %get-tuple-element.11), channel_id=1, source_target_pairs={{0,1},{1,2},{2,3},{3,4},{4,5},{5,6},{6,7},{7,8},{8,9},{9,10},{10,1... | collective-permute-start | bytes 393224 | tf_op jit(solution)/shard_map/ppermute | solution.py:432
  69.0 12.9 %collective-permute-start.2 = (f32[1152,128]{1,0:T(8,128)S(1)}, f32[1152,128]{1,0:T(8,128)S(1)}, u32[]{:S(2)}, u32[]{:S(2)}) collective-permute-start(f32[1152,128]{1,0:T(8,128)S(1)} %get-tuple-element.6), channel_id=1, source_target_pairs={{0,32},{32,64},{64,96},{1,33},{33,65},{65,97},{2,34},{34,66},{66,9... | collective-permute-start | bytes 1769480 | tf_op jit(solution)/shard_map/ppermute | solution.py:432
  75.1 11.2 %collective-permute-start.3 = (f32[1152,128]{1,0:T(8,128)S(1)}, f32[1152,128]{1,0:T(8,128)S(1)}, u32[]{:S(2)}, u32[]{:S(2)}) collective-permute-start(f32[1152,128]{1,0:T(8,128)S(1)} %get-tuple-element.7), channel_id=1, source_target_pairs={{32,0},{64,32},{96,64},{33,1},{65,33},{97,65},{34,2},{66,34},{98,6... | collective-permute-start | bytes 1769480 | tf_op jit(solution)/shard_map/ppermute | solution.py:433

commit v4 on v3

--- a/solution.py
+++ b/solution.py
@@ -68,13 +68,12 @@
         window_kernel,
         out_shape=jax.ShapeDtypeStruct((tiles, planes, wide, 1, LANES), F32),
         in_specs=[anywhere, anywhere],
-        out_specs=pl.BlockSpec(memory_space=pltpu.HBM),
+        out_specs=anywhere,
         scratch_shapes=[
             pltpu.VMEM((planes, lines + 2 * edge, 1, LANES), F32),
             pltpu.SemaphoreType.DMA((2,)),
             pltpu.SemaphoreType.DMA((tiles,)),
         ],
-        compiler_params=pltpu.CompilerParams(vmem_limit_bytes=16 * 2**20),
         name="cut_windows",
     )(strip, depth_plane)
 
@@ -138,7 +137,7 @@
 
 def main_kernel(
     tile, south, north, west, ocean, east, mix_ref, ocean_out, out,
-    raw, stock_a, stock_b, sea, beyond, ocean_a, ocean_b, press, wet, weights, growth0, growth, flat, result, sem,
+    raw, stock_a, stock_b, sea, beyond, ocean_a, ocean_b, press, wet, weights, growth0, growth, flat, held_a, held_b, result, sem,
 ):
     ncp, nrt, ntr = stock_a.shape[0], stock_a.shape[1] - 2, stock_a.shape[2]
     planes = ntr + 1
@@ -319,7 +318,7 @@
         c, x, z, n, s = around(old, cp, q, t)
         return weight[0] * c + weight[1] * x + weight[2] * z + weight[3] * n + weight[4] * s
 
-    def substep(old, first, last, finish):
+    def substep(old, new, first, last, finish):
         for cp in range(first, last):
             for q in range(nrt):
                 p = carry(old, cp, q, 0, [weights[cp, q, k] for k in range(5)])
@@ -334,33 +333,45 @@
 
         blank = jnp.zeros((ROWS8, LANES), F32)
 
-        @pl.loop(first, last)
-        def _(cp):
-            def begin(q):
+        def begin(cp, held):
+            for q in range(nrt):
                 weight = [weights[cp, q, k] for k in range(5)]
-                advected, parts = [], []
+                parts = []
                 for t in range(ntr):
                     a = carry(old, cp, q, t, weight)
-                    advected.append(a)
+                    new[cp, q + 1, t] = a
                     parts.append(a / (saturation + jnp.abs(a)))
                 s = jnp.concatenate(parts + [blank], axis=0)
                 high = s.astype(BF16)
-                low = (s - high.astype(F32)).astype(BF16)
-                return advected, jnp.concatenate([high, low, high], axis=0)
-
-            def end(group, begun):
-                parts = [b[1] for b in begun]
-                s = parts[0] if len(parts) == 1 else jnp.concatenate(parts, axis=1)
+                held[pl.ds(0, deep), pl.ds(q * LANES, LANES)] = high
+                held[pl.ds(deep, deep), pl.ds(q * LANES, LANES)] = (s - high.astype(F32)).astype(BF16)
+
+        def end(cp, held):
+            for q in range(0, nrt, 2):
+                group = range(q, min(q + 2, nrt))
+                across = pl.ds(q * LANES, len(group) * LANES)
+                high = held[pl.ds(0, deep), across]
+                s = jnp.concatenate([high, held[pl.ds(deep, deep), across], high], axis=0)
                 mixed = jnp.dot(mix_all, s, preferred_element_type=F32)
-                for k, q in enumerate(group):
-                    g = growth[cp, q]
+                for k, r in enumerate(group):
+                    g = growth[cp, r]
                     for t in range(ntr):
                         block = mixed[t * ROWS8:(t + 1) * ROWS8, k * LANES:(k + 1) * LANES]
-                        finish(cp, q, t, begun[k][0][t] + g * block)
-
-            for q in range(0, nrt, 2):
-                group = list(range(q, min(q + 2, nrt)))
-                end(group, [begin(r) for r in group])
+                        finish(cp, r, t, new[cp, r + 1, t] + g * block)
+
+        begin(first, held_a)
+
+        @pl.loop(0, (last - first) // 2 - 1)
+        def _(k):
+            cp = first + 2 * k
+            begin(cp + 1, held_b)
+            end(cp, held_a)
+            begin(cp + 2, held_a)
+            end(cp + 1, held_b)
+
+        begin(last - 1, held_b)
+        end(last - 2, held_a)
+        end(last - 1, held_b)
 
     def finish_in(ref):
         def finish(cp, q, t, value):
@@ -374,11 +385,11 @@
 
     edge = halo // 2
     ocean_step(ocean_a, ocean_b, stock_a)
-    substep(stock_a, 0, ncp, finish_in(stock_b))
-    substep(stock_b, edge // 2, ncp - edge // 2, finish_in(stock_a))
+    substep(stock_a, stock_b, 0, ncp, finish_in(stock_b))
+    substep(stock_b, stock_a, edge // 2, ncp - edge // 2, finish_in(stock_a))
     ocean_step(ocean_b, ocean_a, stock_a)
-    substep(stock_a, edge // 2, ncp - edge // 2, finish_in(stock_b))
-    substep(stock_b, edge, ncp - edge, finish_out)
+    substep(stock_a, stock_b, edge // 2, ncp - edge // 2, finish_in(stock_b))
+    substep(stock_b, stock_a, edge, ncp - edge, finish_out)
     send = pltpu.make_async_copy(result.at[pl.ds(halo * ntr * inner, rows * ntr * inner)], out, sem.at[0])
     send.start()
     for f in range(4):
@@ -418,6 +429,8 @@
             pltpu.VMEM((ncp, nrt, ROWS8, LANES), F32),
             pltpu.VMEM((ncp, nrt, ROWS8, LANES), F32),
             pltpu.VMEM((ncp * nrt * ROWS8, LANES), F32),
+            pltpu.VMEM((2 * (ntr + 1) * ROWS8, nrt * LANES), BF16),
+            pltpu.VMEM((2 * (ntr + 1) * ROWS8, nrt * LANES), BF16),
             pltpu.VMEM(((rows + 2 * halo) * ntr * inner, LANES), F32),
             pltpu.SemaphoreType.DMA((1 + 4 * halo,)),
         ],

time: 158 us -> 150 us (0.949)
  Pallas kernels: 37.3 us -> 32.8 us
  local copies, waits for them, and re-layouts: 5.65 us -> 2.74 us
    pallas_call x1, Pallas kernels: 34.3 us -> 27.5 us  [run_window(): pl.pallas_call(main_kernel, out_shape=(jax.ShapeDtypeStruct((4, rows, inn...]
    unnamed x8 -> x4, local copies, waits for them, and re-layouts: 3.59 us -> 0.01 us
    pallas_call x1, Pallas kernels: 1.53 us -> 3.88 us  [cut_windows(): pl.pallas_call(window_kernel, out_shape=jax.ShapeDtypeStruct((tiles, plan...]
where the time goes in v4:
time: 150 us
  waiting for transfers between devices  53.1 us (35%)
  blocking collectives  34.8 us (23%)
  Pallas kernels  32.8 us (22%)
  starting transfers between devices  24.9 us (17%)
  local copies, waits for them, and re-layouts  2.74 us (2%)
    ppermute x2, waiting for transfers between devices, shift(): return lax.ppermute(array, axis, [(i + 1, i) for i in range(count - 1)])  47.2 us
    all_to_all x1, blocking collectives, shards(): lax.all_to_all(result.reshape(tiles, ntr * inner, LANES), 'gx', split_axi...  34.8 us
    pallas_call x1, Pallas kernels, run_window(): pl.pallas_call(main_kernel, out_shape=(jax.ShapeDtypeStruct((4, rows, inn...  27.5 us
    all_to_all x1, starting transfers between devices, shards(): lax.all_to_all(sent.reshape(tiles, planes * ncp, LANES), 'gx', split_axis...  11.6 us
    ppermute x2, starting transfers between devices, shift(): return lax.ppermute(array, axis, [(i, i + 1) for i in range(count - 1)])  10.1 us
    ppermute x2, waiting for transfers between devices, shift(): return lax.ppermute(array, axis, [(i, i + 1) for i in range(count - 1)])  4.88 us
    pallas_call x1, Pallas kernels, cut_windows(): pl.pallas_call(window_kernel, out_shape=jax.ShapeDtypeStruct((tiles, plan...  3.88 us
    ppermute x2, starting transfers between devices, shift(): return lax.ppermute(array, axis, [(i + 1, i) for i in range(count - 1)])  3.21 us
  transfers between devices with their start and end apart: 5, of which 4 were waited for; matrix products, arithmetic and copies ran while one was open for 0% of the time, Pallas kernels for 0%

profile of v4, /device:TPU:1, one launch (start us, length us, event | category | flops | bytes accessed | tf_op | source)
XLA Modules:
  0.0 149.8 jit_solution(7988499470376215658)
XLA Ops:
  0.6 0.7 convert_reduce_fusion
  1.3 0.1 broadcast_in_dim.7
  1.5 0.1 copy.7
  1.6 0.8 copy.8.depth_plane
  2.3 3.9 %cut_windows.1 = f32[32,20,12,1,128]{4,3,2,1,0:T(1,128)} custom-call(f32[19,256,1,128]{3,2,1,0:T(1,128)} %bitcast.12, f32[1,256,1,128]{3,2,1,0:T(1,128)} %copy.8.depth_plane), custom_call_target="tpu_custom_call" | custom-call | tf_op jit(solution)/shard_map/cut_windows/pallas_call | solution.py:67
  6.2 0.0 copy-start
  6.2 11.6 %all-to-all-start = ((f32[32,240,128]{2,1,0:T(8,128)}), f32[32,240,128]{2,1,0:T(8,128)}, u32[]{:S(2)}, u32[]{:S(2)}) async-start(f32[32,240,128]{2,1,0:T(8,128)} %bitcast.10), calls=%async_computation | async-start | bytes 7864320 | tf_op jit(solution)/shard_map/all_to_all | solution.py:467
  17.8 0.0 copy-done
  17.9 0.0 copy-start.1
  17.9 1.3 collective-permute-start.1
  19.2 4.0 %collective-permute-start = (f32[4,32,256]{2,1,0:T(8,128)S(1)}, f32[4,32,256]{2,1,0:T(8,128)S(1)}, u32[]{:S(2)}, u32[]{:S(2)}) collective-permute-start(f32[4,32,256]{2,1,0:T(8,128)S(1)} %get-tuple-element.11), channel_id=1, source_target_pairs={{0,1},{1,2},{2,3},{3,4},{4,5},{5,6},{6,7},{7,8},{8,9},{9,10},{10,1... | collective-permute-start | bytes 393224 | tf_op jit(solution)/shard_map/ppermute | solution.py:445
  23.2 42.9 %collective-permute-done.1.east = f32[4,32,256]{2,1,0:T(8,128)S(1)} collective-permute-done((f32[4,32,256]{2,1,0:T(8,128)S(1)}, f32[4,32,256]{2,1,0:T(8,128)S(1)}, u32[]{:S(2)}, u32[]{:S(2)}) %collective-permute-start.1) | collective-permute-done | bytes 131104 | tf_op jit(solution)/shard_map/ppermute | solution.py:446
  66.0 0.0 collective-permute-done.west
  66.0 1.0 all-to-all-done.tile
  67.0 1.4 row_messages.1
  68.4 6.1 %collective-permute-start.2 = (f32[1152,128]{1,0:T(8,128)S(1)}, f32[1152,128]{1,0:T(8,128)S(1)}, u32[]{:S(2)}, u32[]{:S(2)}) collective-permute-start(f32[1152,128]{1,0:T(8,128)S(1)} %get-tuple-element.6), channel_id=1, source_target_pairs={{0,32},{32,64},{64,96},{1,33},{33,65},{65,97},{2,34},{34,66},{66,9... | collective-permute-start | bytes 1769480 | tf_op jit(solution)/shard_map/ppermute | solution.py:445
  74.5 1.9 %collective-permute-start.3 = (f32[1152,128]{1,0:T(8,128)S(1)}, f32[1152,128]{1,0:T(8,128)S(1)}, u32[]{:S(2)}, u32[]{:S(2)}) collective-permute-start(f32[1152,128]{1,0:T(8,128)S(1)} %get-tuple-element.7), channel_id=1, source_target_pairs={{32,0},{64,32},{96,64},{33,1},{65,33},{97,65},{34,2},{66,34},{98,6... | collective-permute-start | bytes 1769480 | tf_op jit(solution)/shard_map/ppermute | solution.py:446
  76.5 4.9 %collective-permute-done.2.south = f32[1152,128]{1,0:T(8,128)S(1)} collective-permute-done((f32[1152,128]{1,0:T(8,128)S(1)}, f32[1152,128]{1,0:T(8,128)S(1)}, u32[]{:S(2)}, u32[]{:S(2)}) %collective-permute-start.2) | collective-permute-done | bytes 589856 | tf_op jit(solution)/shard_map/ppermute | solution.py:445
  81.3 4.4 %collective-permute-done.3.north = f32[1152,128]{1,0:T(8,128)S(1)} collective-permute-done((f32[1152,128]{1,0:T(8,128)S(1)}, f32[1152,128]{1,0:T(8,128)S(1)}, u32[]{:S(2)}, u32[]{:S(2)}) %collective-permute-start.3) | collective-permute-done | bytes 589856 | tf_op jit(solution)/shard_map/ppermute | solution.py:446
  85.7 0.0 copy-done.1
  85.7 27.5 %window.1 = (f32[4,32,1024]{2,1,0:T(8,128)}, f32[4864,128]{1,0:T(8,128)S(1)}) custom-call(f32[7680,128]{1,0:T(8,128)} %bitcast.3.tile, f32[1152,128]{1,0:T(8,128)S(1)} %collective-permute-done.2.south, f32[1152,128]{1,0:T(8,128)S(1)} %collective-permute-done.3.north, f32[4,32,256]{2,1,0:T(8,128)S(1)} %collective-permute-done.west, ...), custom_call_target="tpu_custom_call" | custom-call | tf_op jit(solution)/shard_map/window/pallas_call | solution.py:410
  113.3 34.8 %all_to_all.10 = f32[32,152,128]{2,1,0:T(8,128)S(1)} all-to-all(f32[32,152,128]{2,1,0:T(8,128)S(1)} %bitcast.9), channel_id=1, replica_groups=mesh['grp'=4,'gx'=32] {'gx'}, dimensions={0} | all-to-all | bytes 4980736 | tf_op jit(solution)/shard_map/all_to_all | solution.py:474
  148.1 1.7 %copy.9 = f32[32,19,8,128]{3,2,0,1:T(8,128)} copy(f32[32,19,8,128]{3,2,1,0:T(8,128)S(1)} %bitcast.11) | data formatting | bytes 4980736 | tf_op jit(solution)/shard_map/reshape | solution.py:475
  (2 shorter events, 0.0 us)
Async XLA Ops:
  6.2 11.6 %copy-start = (f32[4,32,1024]{2,1,0:T(8,128)S(1)}, f32[4,32,1024]{2,1,0:T(8,128)}, u32[]{:S(2)}) copy-start(f32[4,32,1024]{2,1,0:T(8,128)} %ocean.3) | copy-start | bytes 1572868
  6.2 60.8 %all-to-all-start = ((f32[32,240,128]{2,1,0:T(8,128)}), f32[32,240,128]{2,1,0:T(8,128)}, u32[]{:S(2)}, u32[]{:S(2)}) async-start(f32[32,240,128]{2,1,0:T(8,128)} %bitcast.10), calls=%async_computation | async-start | bytes 7864320 | tf_op jit(solution)/shard_map/all_to_all | solution.py:467
  17.9 67.9 %copy-start.1 = (f32[19,19]{1,0:T(8,128)S(1)}, f32[19,19]{1,0:T(8,128)}, u32[]{:S(2)}) copy-start(f32[19,19]{1,0:T(8,128)} %mix_ref.1) | copy-start | bytes 4336
  17.9 48.2 %collective-permute-start.1 = (f32[4,32,256]{2,1,0:T(8,128)S(1)}, f32[4,32,256]{2,1,0:T(8,128)S(1)}, u32[]{:S(2)}, u32[]{:S(2)}) collective-permute-start(f32[4,32,256]{2,1,0:T(8,128)S(1)} %get-tuple-element.10), channel_id=1, source_target_pairs={{1,0},{2,1},{3,2},{4,3},{5,4},{6,5},{7,6},{8,7},{9,8},{10,9},{11,1... | collective-permute-start | bytes 393224 | tf_op jit(solution)/shard_map/ppermute | solution.py:446
  19.2 46.9 %collective-permute-start = (f32[4,32,256]{2,1,0:T(8,128)S(1)}, f32[4,32,256]{2,1,0:T(8,128)S(1)}, u32[]{:S(2)}, u32[]{:S(2)}) collective-permute-start(f32[4,32,256]{2,1,0:T(8,128)S(1)} %get-tuple-element.11), channel_id=1, source_target_pairs={{0,1},{1,2},{2,3},{3,4},{4,5},{5,6},{6,7},{7,8},{8,9},{9,10},{10,1... | collective-permute-start | bytes 393224 | tf_op jit(solution)/shard_map/ppermute | solution.py:445
  68.4 12.9 %collective-permute-start.2 = (f32[1152,128]{1,0:T(8,128)S(1)}, f32[1152,128]{1,0:T(8,128)S(1)}, u32[]{:S(2)}, u32[]{:S(2)}) collective-permute-start(f32[1152,128]{1,0:T(8,128)S(1)} %get-tuple-element.6), channel_id=1, source_target_pairs={{0,32},{32,64},{64,96},{1,33},{33,65},{65,97},{2,34},{34,66},{66,9... | collective-permute-start | bytes 1769480 | tf_op jit(solution)/shard_map/ppermute | solution.py:445
  74.5 11.2 %collective-permute-start.3 = (f32[1152,128]{1,0:T(8,128)S(1)}, f32[1152,128]{1,0:T(8,128)S(1)}, u32[]{:S(2)}, u32[]{:S(2)}) collective-permute-start(f32[1152,128]{1,0:T(8,128)S(1)} %get-tuple-element.7), channel_id=1, source_target_pairs={{32,0},{64,32},{96,64},{33,1},{65,33},{97,65},{34,2},{66,34},{98,6... | collective-permute-start | bytes 1769480 | tf_op jit(solution)/shard_map/ppermute | solution.py:446

commit v5 on v4

--- a/solution.py
+++ b/solution.py
@@ -32,66 +32,86 @@
 BF16 = jnp.bfloat16
 
 
-def window_kernel(strip, depth_plane, out, big, sem_in, sem_out):
-    planes, lines = big.shape[0], strip.shape[1]
-    tiles, wide = out.shape[0], out.shape[2]
+GROUP = 4
+PIECES = 4
+
+
+def window_kernel(strip, depth_lines, out, big, depth, sem_in, sem_out):
+    ntr, lines = strip.shape[0], strip.shape[1]
+    tiles, groups = out.shape[0], (out.shape[1] - 1) // ntr
     step = lines // tiles
-    edge = (wide - step) // 2
-    tracers_in = pltpu.make_async_copy(strip, big.at[pl.ds(0, planes - 1), pl.ds(edge, lines)], sem_in.at[0])
-    depth_in = pltpu.make_async_copy(depth_plane, big.at[pl.ds(planes - 1, 1), pl.ds(edge, lines)], sem_in.at[1])
-    tracers_in.start()
-    depth_in.start()
-    zeros = jnp.zeros((planes, edge, 1, LANES), F32)
+    edge = (big.shape[1] - lines) // 2
+    span = lines // PIECES
+    arrivals = [
+        pltpu.make_async_copy(strip.at[:, pl.ds(p * span, span)], big.at[:, pl.ds(edge + p * span, span)], sem_in.at[p])
+        for p in range(PIECES)
+    ]
+    depth_in = pltpu.make_async_copy(depth_lines, depth, sem_in.at[PIECES])
+    for copy in [depth_in] + arrivals:
+        copy.start()
+    zeros = jnp.zeros((ntr, edge, 1, LANES), F32)
     big[:, pl.ds(0, edge)] = zeros
     big[:, pl.ds(edge + lines, edge)] = zeros
-    tracers_in.wait()
+
+    def sends(d):
+        window = [
+            pltpu.make_async_copy(
+                big.at[:, pl.ds(d * step + g * GROUP, GROUP)], out.at[d, pl.ds(g * ntr, ntr)], sem_out.at[d, g]
+            )
+            for g in range(groups)
+        ]
+        return window + [pltpu.make_async_copy(depth.at[d], out.at[d, groups * ntr], sem_out.at[d, groups])]
+
     depth_in.wait()
-
-    def send(d):
-        return pltpu.make_async_copy(big.at[:, pl.ds(d * step, wide)], out.at[d], sem_out.at[d])
+    first = 0
+    for p in range(PIECES):
+        arrivals[p].wait()
+        last = tiles if p == PIECES - 1 else (span * (p + 1) + edge - groups * GROUP) // step + 1
+
+        @pl.loop(first, last)
+        def _(d):
+            for copy in sends(d):
+                copy.start()
+
+        first = last
 
     @pl.loop(0, tiles)
     def _(d):
-        send(d).start()
-
-    @pl.loop(0, tiles)
-    def _(d):
-        send(d).wait()
-
-
-def cut_windows(strip, depth_plane, tiles, wide):
-    planes = strip.shape[0] + 1
-    lines = strip.shape[1]
+        for copy in sends(d):
+            copy.wait()
+
+
+def cut_windows(strip, depth_lines, tiles, wide):
+    ntr, lines = strip.shape[0], strip.shape[1]
+    groups = wide // GROUP
     edge = (wide - lines // tiles) // 2
     anywhere = pl.BlockSpec(memory_space=pl.ANY)
     return pl.pallas_call(
         window_kernel,
-        out_shape=jax.ShapeDtypeStruct((tiles, planes, wide, 1, LANES), F32),
+        out_shape=jax.ShapeDtypeStruct((tiles, groups * ntr + 1, GROUP, 1, LANES), F32),
         in_specs=[anywhere, anywhere],
         out_specs=anywhere,
         scratch_shapes=[
-            pltpu.VMEM((planes, lines + 2 * edge, 1, LANES), F32),
-            pltpu.SemaphoreType.DMA((2,)),
-            pltpu.SemaphoreType.DMA((tiles,)),
+            pltpu.VMEM((ntr, lines + 2 * edge, 1, LANES), F32),
+            pltpu.VMEM((tiles, GROUP, 1, LANES), F32),
+            pltpu.SemaphoreType.DMA((PIECES + 1,)),
+            pltpu.SemaphoreType.DMA((tiles, groups + 1)),
         ],
         name="cut_windows",
-    )(strip, depth_plane)
+    )(strip, depth_lines)
 
 
 def edge_kernel(tile, west, ocean, east, to_north, to_south, lines, sem):
-    planes_lines = tile.shape[1]
     rows = ocean.shape[1]
     halo = HALO
     wide = lines.shape[1] // halo
+    per_row = tile.shape[0] // rows
     sides = ((to_north, rows - halo), (to_south, 0))
     copies = [
         pltpu.make_async_copy(
-            tile.at[first + r],
-            message.at[pl.ds(r * (planes_lines + wide), planes_lines)],
-            sem.at[k * halo + r],
+            tile.at[pl.ds(first * per_row, halo * per_row)], message.at[pl.ds(0, halo * per_row)], sem.at[k]
         )
         for k, (message, first) in enumerate(sides)
-        for r in range(halo)
     ]
     for copy in copies:
         copy.start()
@@ -103,13 +123,8 @@
                     lines[k, pl.ds(c, halo, stride=wide), :] = part[f, pl.ds(first, halo), pl.ds(j * LANES, LANES)]
                     c += 1
     more = [
-        pltpu.make_async_copy(
-            lines.at[k, pl.ds(r * wide, wide)],
-            message.at[pl.ds(r * (planes_lines + wide) + planes_lines, wide)],
-            sem.at[(2 + k) * halo + r],
-        )
+        pltpu.make_async_copy(lines.at[k], message.at[pl.ds(halo * per_row, halo * wide)], sem.at[2 + k])
         for k, (message, first) in enumerate(sides)
-        for r in range(halo)
     ]
     for copy in more:
         copy.start()
@@ -120,7 +135,7 @@
 def row_messages(tile, west, ocean, east, ncp):
     anywhere = pl.BlockSpec(memory_space=pl.ANY)
     inside = pl.BlockSpec(memory_space=pltpu.VMEM)
-    message = jax.ShapeDtypeStruct((HALO * (tile.shape[1] + 4 * ncp), LANES), F32)
+    message = jax.ShapeDtypeStruct((HALO * (tile.shape[0] // ocean.shape[1] + 4 * ncp), LANES), F32)
     return pl.pallas_call(
         edge_kernel,
         out_shape=(message, message),
@@ -128,7 +143,7 @@
         out_specs=(anywhere, anywhere),
         scratch_shapes=[
             pltpu.VMEM((2, HALO * 4 * ncp, LANES), F32),
-            pltpu.SemaphoreType.DMA((4 * HALO,)),
+            pltpu.SemaphoreType.DMA((4,)),
         ],
         compiler_params=pltpu.CompilerParams(vmem_limit_bytes=8 * 2**20),
         name="row_messages",
@@ -140,27 +155,20 @@
     raw, stock_a, stock_b, sea, beyond, ocean_a, ocean_b, press, wet, weights, growth0, growth, flat, held_a, held_b, result, sem,
 ):
     ncp, nrt, ntr = stock_a.shape[0], stock_a.shape[1] - 2, stock_a.shape[2]
-    planes = ntr + 1
-    line_stride = planes * ncp
-    rows = tile.shape[0] // line_stride
+    rows = ocean.shape[1]
+    line_stride = tile.shape[0] // rows
+    groups = ncp // GROUP
     halo = HALO
     inner = ncp - halo
     wide_ocean = 4 * ncp
+    many = halo * line_stride
     copies = [
-        pltpu.make_async_copy(tile, raw.at[pl.ds(halo * line_stride, rows * line_stride)], sem.at[0]),
+        pltpu.make_async_copy(tile, raw.at[pl.ds(many, rows * line_stride)], sem.at[0]),
+        pltpu.make_async_copy(south.at[pl.ds(0, many)], raw.at[pl.ds(0, many)], sem.at[1]),
+        pltpu.make_async_copy(north.at[pl.ds(0, many)], raw.at[pl.ds((halo + rows) * line_stride, many)], sem.at[2]),
+        pltpu.make_async_copy(south.at[pl.ds(many, halo * wide_ocean)], beyond.at[0], sem.at[3]),
+        pltpu.make_async_copy(north.at[pl.ds(many, halo * wide_ocean)], beyond.at[1], sem.at[4]),
     ]
-    for side, message in enumerate((south, north)):
-        for r in range(halo):
-            start = r * (line_stride + wide_ocean)
-            row = r + side * (halo + rows)
-            copies.append(pltpu.make_async_copy(
-                message.at[pl.ds(start, line_stride)], raw.at[pl.ds(row * line_stride, line_stride)],
-                sem.at[len(copies)],
-            ))
-            copies.append(pltpu.make_async_copy(
-                message.at[pl.ds(start + line_stride, wide_ocean)], beyond.at[side, pl.ds(r * wide_ocean, wide_ocean)],
-                sem.at[len(copies)],
-            ))
     for copy in copies:
         copy.start()
 
@@ -239,14 +247,22 @@
             for q in range(nrt):
                 put(ocean_a, cp, q, sea[f, cp, pl.ds(q, ROWS8, stride=nrt), :], f)
 
+    def spaced(start):
+        return pl.ds(start, ROWS8, stride=nrt * line_stride)
+
+    depths = jnp.concatenate(
+        [raw[spaced(q * line_stride + groups * ntr * GROUP), :] for q in range(nrt)] + [jnp.zeros((ROWS8, LANES), F32)], axis=0
+    ).astype(BF16)
+
     @pl.loop(0, ncp)
     def _(cp):
+        of_pair = (row_id == 2 * cp + col_id // half).astype(F32).astype(BF16)
+        depth = jnp.dot(depths, of_pair, preferred_element_type=F32)
         for q in range(nrt):
-            base = q * line_stride + cp
+            base = q * line_stride + (cp // GROUP) * (ntr * GROUP) + cp % GROUP
             for t in range(ntr):
-                put(stock_a, cp, q, raw[pl.ds(base + t * ncp, ROWS8, stride=nrt * line_stride), :], t)
-            depth = raw[pl.ds(base + ntr * ncp, ROWS8, stride=nrt * line_stride), :]
-            put(wet, cp, q, (level_f < depth).astype(F32))
+                put(stock_a, cp, q, raw[spaced(base + t * GROUP), :], t)
+            put(wet, cp, q, (level_f < depth[q * ROWS8:(q + 1) * ROWS8]).astype(F32))
 
     first_row = lax.axis_index("grp") * rows - halo
     total_rows = rows * lax.axis_size("grp")
@@ -416,7 +432,7 @@
         in_specs=[anywhere] * 3 + [inside] * 4,
         out_specs=(inside, anywhere),
         scratch_shapes=[
-            pltpu.VMEM(((rows + 2 * halo) * (ntr + 1) * ncp, LANES), F32),
+            pltpu.VMEM(((rows + 2 * halo) * (tile.shape[0] // rows), LANES), F32),
             pltpu.VMEM((ncp, nrt + 2, ntr, ROWS8, LANES), F32),
             pltpu.VMEM((ncp, nrt + 2, ntr, ROWS8, LANES), F32),
             pltpu.VMEM((4, ncp, rows + 2 * halo, LANES), F32),
@@ -432,7 +448,7 @@
             pltpu.VMEM((2 * (ntr + 1) * ROWS8, nrt * LANES), BF16),
             pltpu.VMEM((2 * (ntr + 1) * ROWS8, nrt * LANES), BF16),
             pltpu.VMEM(((rows + 2 * halo) * ntr * inner, LANES), F32),
-            pltpu.SemaphoreType.DMA((1 + 4 * halo,)),
+            pltpu.SemaphoreType.DMA((5,)),
         ],
         compiler_params=pltpu.CompilerParams(vmem_limit_bytes=40 * 2**20),
         name="window",
@@ -457,19 +473,29 @@
     inner = lines // tiles
     edge = HALO // pair
     ncp = inner + 2 * edge
-    planes = ntr + 1
 
     margin = edge * LANES
     from_west = shift(ocean_fields[:, :, -margin:], "gx", 1)
     from_east = shift(ocean_fields[:, :, :margin], "gx", -1)
-    depth = jnp.broadcast_to(wet_levels.astype(F32).reshape(lines, pair, 1), (lines, pair, levels))
-    sent = cut_windows(tracers.reshape(ntr, lines, 1, LANES), depth.reshape(1, lines, 1, LANES), tiles, ncp)
-    tile = lax.all_to_all(sent.reshape(tiles, planes * ncp, LANES), "gx", split_axis=0, concat_axis=0, tiled=True)
+    depth = wet_levels.astype(F32).reshape(tiles, columns // tiles)
+    blank = jnp.zeros((1, HALO), F32)
+    depth = jnp.concatenate(
+        [
+            jnp.concatenate([blank, depth[:-1, -HALO:]], axis=0),
+            depth,
+            jnp.concatenate([depth[1:, :HALO], blank], axis=0),
+            jnp.zeros((tiles, GROUP * LANES - columns // tiles - 2 * HALO), F32),
+        ],
+        axis=1,
+    )
+    sent = cut_windows(tracers.reshape(ntr, lines, 1, LANES), depth.reshape(tiles, GROUP, 1, LANES), tiles, ncp)
+    tile = lax.all_to_all(sent.reshape(tiles, -1, LANES), "gx", split_axis=0, concat_axis=0, tiled=True)
+    tile = tile.reshape(-1, LANES)
     to_north, to_south = row_messages(tile, from_west, ocean_fields, from_east, ncp)
     south = shift(to_north, "grp", 1)
     north = shift(to_south, "grp", -1)
     ocean_next, result = run_window(
-        tile.reshape(-1, LANES), south, north, from_west, ocean_fields, from_east, interaction, ntr, ncp
+        tile, south, north, from_west, ocean_fields, from_east, interaction, ntr, ncp
     )
     back = lax.all_to_all(result.reshape(tiles, ntr * inner, LANES), "gx", split_axis=0, concat_axis=0, tiled=True)
     back = back.reshape(tiles, ntr, inner, LANES).transpose(1, 0, 2, 3)

time: 150 us -> 148 us (0.987)
  waiting for transfers between devices: 53.1 us -> 51.2 us
    ppermute x2, waiting for transfers between devices: 47.2 us -> 45.4 us  [shift(): return lax.ppermute(array, axis, [(i + 1, i) for i in range(count - 1)])]
where the time goes in v5:
time: 148 us; the launch traced here: 147 us
  waiting for transfers between devices  51.2 us (35%)
  blocking collectives  34.4 us (23%)
  Pallas kernels  32.7 us (22%)
  starting transfers between devices  24.8 us (17%)
  local copies, waits for them, and re-layouts  2.69 us (2%)
    ppermute x2, waiting for transfers between devices, shift(): return lax.ppermute(array, axis, [(i + 1, i) for i in range(count - 1)])  45.4 us
    all_to_all x1, blocking collectives, shards(): lax.all_to_all(result.reshape(tiles, ntr * inner, LANES), 'gx', split_axi...  34.4 us
    pallas_call x1, Pallas kernels, run_window(): pl.pallas_call(main_kernel, out_shape=(jax.ShapeDtypeStruct((4, rows, inn...  27.3 us
    all_to_all x1, starting transfers between devices, shards(): lax.all_to_all(sent.reshape(tiles, -1, LANES), 'gx', split_axis=0, concat...  11.6 us
    ppermute x2, starting transfers between devices, shift(): return lax.ppermute(array, axis, [(i, i + 1) for i in range(count - 1)])  10 us
    ppermute x2, waiting for transfers between devices, shift(): return lax.ppermute(array, axis, [(i, i + 1) for i in range(count - 1)])  4.7 us
    pallas_call x1, Pallas kernels, cut_windows(): pl.pallas_call(window_kernel, out_shape=jax.ShapeDtypeStruct((tiles, grou...  4.19 us
    ppermute x2, starting transfers between devices, shift(): return lax.ppermute(array, axis, [(i + 1, i) for i in range(count - 1)])  3.21 us
  transfers between devices with their start and end apart: 5, of which 4 were waited for; matrix products, arithmetic and copies ran while one was open for 0% of the time, Pallas kernels for 0%

profile of v5, /device:TPU:1, one launch (start us, length us, event | category | flops | bytes accessed | tf_op | source)
XLA Modules:
  0.0 147.3 jit_solution(2206266705487288445)
XLA Ops:
  0.6 0.7 convert_reduce_fusion
  1.3 0.1 reshape.29
  1.4 0.1 fusion.3
  1.5 0.1 pad.5.clone
  1.6 0.1 fusion
  1.7 0.7 reshape.30.depth_lines
  2.4 4.2 %cut_windows.1 = f32[32,58,4,1,128]{4,3,2,1,0:T(1,128)} custom-call(f32[19,256,1,128]{3,2,1,0:T(1,128)} %bitcast.11, f32[32,4,1,128]{3,2,1,0:T(1,128)} %reshape.30.depth_lines), custom_call_target="tpu_custom_call" | custom-call | tf_op jit(solution)/shard_map/cut_windows/pallas_call | solution.py:89
  6.6 0.0 copy-start
  6.6 11.6 %all-to-all-start = ((f32[32,232,128]{2,1,0:T(8,128)}), f32[32,232,128]{2,1,0:T(8,128)}, u32[]{:S(2)}, u32[]{:S(2)}) async-start(f32[32,232,128]{2,1,0:T(8,128)} %bitcast.9), calls=%async_computation | async-start | bytes 7602176 | tf_op jit(solution)/shard_map/all_to_all | solution.py:492
  18.2 0.0 copy-done
  18.2 0.0 copy-start.1
  18.2 1.3 collective-permute-start.1
  19.5 4.0 %collective-permute-start = (f32[4,32,256]{2,1,0:T(8,128)S(1)}, f32[4,32,256]{2,1,0:T(8,128)S(1)}, u32[]{:S(2)}, u32[]{:S(2)}) collective-permute-start(f32[4,32,256]{2,1,0:T(8,128)S(1)} %get-tuple-element.11), channel_id=1, source_target_pairs={{0,1},{1,2},{2,3},{3,4},{4,5},{5,6},{6,7},{7,8},{8,9},{9,10},{10,1... | collective-permute-start | bytes 393224 | tf_op jit(solution)/shard_map/ppermute | solution.py:461
  23.5 41.0 %collective-permute-done.1.east = f32[4,32,256]{2,1,0:T(8,128)S(1)} collective-permute-done((f32[4,32,256]{2,1,0:T(8,128)S(1)}, f32[4,32,256]{2,1,0:T(8,128)S(1)}, u32[]{:S(2)}, u32[]{:S(2)}) %collective-permute-start.1) | collective-permute-done | bytes 131104 | tf_op jit(solution)/shard_map/ppermute | solution.py:462
  64.5 0.0 collective-permute-done.west
  64.6 1.0 all-to-all-done
  65.6 1.2 row_messages.1
  66.8 6.0 %collective-permute-start.2 = (f32[1120,128]{1,0:T(8,128)S(1)}, f32[1120,128]{1,0:T(8,128)S(1)}, u32[]{:S(2)}, u32[]{:S(2)}) collective-permute-start(f32[1120,128]{1,0:T(8,128)S(1)} %get-tuple-element.6), channel_id=1, source_target_pairs={{0,32},{32,64},{64,96},{1,33},{33,65},{65,97},{2,34},{34,66},{66,9... | collective-permute-start | bytes 1720328 | tf_op jit(solution)/shard_map/ppermute | solution.py:461
  72.9 1.9 %collective-permute-start.3 = (f32[1120,128]{1,0:T(8,128)S(1)}, f32[1120,128]{1,0:T(8,128)S(1)}, u32[]{:S(2)}, u32[]{:S(2)}) collective-permute-start(f32[1120,128]{1,0:T(8,128)S(1)} %get-tuple-element.7), channel_id=1, source_target_pairs={{32,0},{64,32},{96,64},{33,1},{65,33},{97,65},{34,2},{66,34},{98,6... | collective-permute-start | bytes 1720328 | tf_op jit(solution)/shard_map/ppermute | solution.py:462
  74.8 4.7 %collective-permute-done.2.south = f32[1120,128]{1,0:T(8,128)S(1)} collective-permute-done((f32[1120,128]{1,0:T(8,128)S(1)}, f32[1120,128]{1,0:T(8,128)S(1)}, u32[]{:S(2)}, u32[]{:S(2)}) %collective-permute-start.2) | collective-permute-done | bytes 573472 | tf_op jit(solution)/shard_map/ppermute | solution.py:461
  79.5 4.4 %collective-permute-done.3.north = f32[1120,128]{1,0:T(8,128)S(1)} collective-permute-done((f32[1120,128]{1,0:T(8,128)S(1)}, f32[1120,128]{1,0:T(8,128)S(1)}, u32[]{:S(2)}, u32[]{:S(2)}) %collective-permute-start.3) | collective-permute-done | bytes 573472 | tf_op jit(solution)/shard_map/ppermute | solution.py:462
  83.9 0.0 copy-done.1
  83.9 27.3 %window.1 = (f32[4,32,1024]{2,1,0:T(8,128)}, f32[4864,128]{1,0:T(8,128)S(1)}) custom-call(f32[7424,128]{1,0:T(8,128)} %bitcast.2.tile, f32[1120,128]{1,0:T(8,128)S(1)} %collective-permute-done.2.south, f32[1120,128]{1,0:T(8,128)S(1)} %collective-permute-done.3.north, f32[4,32,256]{2,1,0:T(8,128)S(1)} %collective-permute-done.west, ...), custom_call_target="tpu_custom_call" | custom-call | tf_op jit(solution)/shard_map/window/pallas_call | solution.py:426
  111.2 34.4 %all_to_all.10 = f32[32,152,128]{2,1,0:T(8,128)S(1)} all-to-all(f32[32,152,128]{2,1,0:T(8,128)S(1)} %bitcast.8), channel_id=1, replica_groups=mesh['grp'=4,'gx'=32] {'gx'}, dimensions={0} | all-to-all | bytes 4980736 | tf_op jit(solution)/shard_map/all_to_all | solution.py:500
  145.6 1.7 %copy.7 = f32[32,19,8,128]{3,2,0,1:T(8,128)} copy(f32[32,19,8,128]{3,2,1,0:T(8,128)S(1)} %bitcast.10) | data formatting | bytes 4980736 | tf_op jit(solution)/shard_map/reshape | solution.py:501
  (2 shorter events, 0.0 us)
Async XLA Ops:
  6.6 11.6 %copy-start = (f32[4,32,1024]{2,1,0:T(8,128)S(1)}, f32[4,32,1024]{2,1,0:T(8,128)}, u32[]{:S(2)}) copy-start(f32[4,32,1024]{2,1,0:T(8,128)} %ocean.3) | copy-start | bytes 1572868
  6.6 59.0 %all-to-all-start = ((f32[32,232,128]{2,1,0:T(8,128)}), f32[32,232,128]{2,1,0:T(8,128)}, u32[]{:S(2)}, u32[]{:S(2)}) async-start(f32[32,232,128]{2,1,0:T(8,128)} %bitcast.9), calls=%async_computation | async-start | bytes 7602176 | tf_op jit(solution)/shard_map/all_to_all | solution.py:492
  18.2 65.7 %copy-start.1 = (f32[19,19]{1,0:T(8,128)S(1)}, f32[19,19]{1,0:T(8,128)}, u32[]{:S(2)}) copy-start(f32[19,19]{1,0:T(8,128)} %mix_ref.1) | copy-start | bytes 4336
  18.2 46.3 %collective-permute-start.1 = (f32[4,32,256]{2,1,0:T(8,128)S(1)}, f32[4,32,256]{2,1,0:T(8,128)S(1)}, u32[]{:S(2)}, u32[]{:S(2)}) collective-permute-start(f32[4,32,256]{2,1,0:T(8,128)S(1)} %get-tuple-element.10), channel_id=1, source_target_pairs={{1,0},{2,1},{3,2},{4,3},{5,4},{6,5},{7,6},{8,7},{9,8},{10,9},{11,1... | collective-permute-start | bytes 393224 | tf_op jit(solution)/shard_map/ppermute | solution.py:462
  19.5 45.0 %collective-permute-start = (f32[4,32,256]{2,1,0:T(8,128)S(1)}, f32[4,32,256]{2,1,0:T(8,128)S(1)}, u32[]{:S(2)}, u32[]{:S(2)}) collective-permute-start(f32[4,32,256]{2,1,0:T(8,128)S(1)} %get-tuple-element.11), channel_id=1, source_target_pairs={{0,1},{1,2},{2,3},{3,4},{4,5},{5,6},{6,7},{7,8},{8,9},{9,10},{10,1... | collective-permute-start | bytes 393224 | tf_op jit(solution)/shard_map/ppermute | solution.py:461
  66.8 12.7 %collective-permute-start.2 = (f32[1120,128]{1,0:T(8,128)S(1)}, f32[1120,128]{1,0:T(8,128)S(1)}, u32[]{:S(2)}, u32[]{:S(2)}) collective-permute-start(f32[1120,128]{1,0:T(8,128)S(1)} %get-tuple-element.6), channel_id=1, source_target_pairs={{0,32},{32,64},{64,96},{1,33},{33,65},{65,97},{2,34},{34,66},{66,9... | collective-permute-start | bytes 1720328 | tf_op jit(solution)/shard_map/ppermute | solution.py:461
  72.9 11.0 %collective-permute-start.3 = (f32[1120,128]{1,0:T(8,128)S(1)}, f32[1120,128]{1,0:T(8,128)S(1)}, u32[]{:S(2)}, u32[]{:S(2)}) collective-permute-start(f32[1120,128]{1,0:T(8,128)S(1)} %get-tuple-element.7), channel_id=1, source_target_pairs={{32,0},{64,32},{96,64},{33,1},{65,33},{97,65},{34,2},{66,34},{98,6... | collective-permute-start | bytes 1720328 | tf_op jit(solution)/shard_map/ppermute | solution.py:462

commit v6 on v5

--- a/solution.py
+++ b/solution.py
@@ -36,7 +36,7 @@
 PIECES = 4
 
 
-def window_kernel(strip, depth_lines, out, big, depth, sem_in, sem_out):
+def window_kernel(strip, wet_levels, out, big, depth, sem_in, sem_out):
     ntr, lines = strip.shape[0], strip.shape[1]
     tiles, groups = out.shape[0], (out.shape[1] - 1) // ntr
     step = lines // tiles
@@ -46,23 +46,22 @@
         pltpu.make_async_copy(strip.at[:, pl.ds(p * span, span)], big.at[:, pl.ds(edge + p * span, span)], sem_in.at[p])
         for p in range(PIECES)
     ]
-    depth_in = pltpu.make_async_copy(depth_lines, depth, sem_in.at[PIECES])
-    for copy in [depth_in] + arrivals:
+    for copy in arrivals:
         copy.start()
     zeros = jnp.zeros((ntr, edge, 1, LANES), F32)
     big[:, pl.ds(0, edge)] = zeros
     big[:, pl.ds(edge + lines, edge)] = zeros
 
     def sends(d):
-        window = [
+        return [
             pltpu.make_async_copy(
                 big.at[:, pl.ds(d * step + g * GROUP, GROUP)], out.at[d, pl.ds(g * ntr, ntr)], sem_out.at[d, g]
             )
             for g in range(groups)
         ]
-        return window + [pltpu.make_async_copy(depth.at[d], out.at[d, groups * ntr], sem_out.at[d, groups])]
-
-    depth_in.wait()
+
+    depth_out = pltpu.make_async_copy(depth, out.at[:, groups * ntr], sem_in.at[PIECES])
+
     first = 0
     for p in range(PIECES):
         arrivals[p].wait()
@@ -75,13 +74,24 @@
 
         first = last
 
+    columns = wet_levels.shape[1]
+    depth[...] = jnp.zeros(depth.shape, F32)
+    around = jnp.concatenate(
+        [jnp.zeros((1, HALO), F32), wet_levels[...].astype(F32), jnp.zeros((1, LANES - HALO), F32)], axis=1
+    )
+    for d in range(tiles):
+        depth[d, 0] = around[:, d * (columns // tiles):d * (columns // tiles) + LANES]
+    depth_out.start()
+
     @pl.loop(0, tiles)
     def _(d):
         for copy in sends(d):
             copy.wait()
 
-
-def cut_windows(strip, depth_lines, tiles, wide):
+    depth_out.wait()
+
+
+def cut_windows(strip, wet_levels, tiles, wide):
     ntr, lines = strip.shape[0], strip.shape[1]
     groups = wide // GROUP
     edge = (wide - lines // tiles) // 2
@@ -89,16 +99,16 @@
     return pl.pallas_call(
         window_kernel,
         out_shape=jax.ShapeDtypeStruct((tiles, groups * ntr + 1, GROUP, 1, LANES), F32),
-        in_specs=[anywhere, anywhere],
+        in_specs=[anywhere, pl.BlockSpec(memory_space=pltpu.VMEM)],
         out_specs=anywhere,
         scratch_shapes=[
             pltpu.VMEM((ntr, lines + 2 * edge, 1, LANES), F32),
             pltpu.VMEM((tiles, GROUP, 1, LANES), F32),
             pltpu.SemaphoreType.DMA((PIECES + 1,)),
-            pltpu.SemaphoreType.DMA((tiles, groups + 1)),
+            pltpu.SemaphoreType.DMA((tiles, groups)),
         ],
         name="cut_windows",
-    )(strip, depth_lines)
+    )(strip, wet_levels)
 
 
 def edge_kernel(tile, west, ocean, east, to_north, to_south, lines, sem):
@@ -270,7 +280,7 @@
     def line(cp, q):
         return pl.ds((cp * nrt + q) * ROWS8, ROWS8)
 
-    def ocean_step(old, new, stock):
+    def ocean_step(old, new, stock, first, last):
         for cp in range(ncp):
             for q in range(nrt):
                 flat[line(cp, q), :] = (haline * old[cp, q + 1, 3] - thermal * old[cp, q + 1, 2]) * wet[cp, q + 1]
@@ -278,13 +288,14 @@
         for cp in range(ncp):
             for q in range(nrt):
                 put(press, cp, q, flat[line(cp, q), :])
-        for cp in range(ncp):
+        for cp in range(first, last):
             for q in range(nrt):
                 flat[line(cp, q), :] = water_extinction + pigment_extinction * stock[cp, q + 1, 0]
-        extinct_all = flat[...]
-        flat[...] = heating_rate * extinct_all * jnp.exp(-(running_sums(extinct_all) - 0.5 * extinct_all))
-
-        @pl.loop(0, ncp)
+        span = pl.ds(first * nrt * ROWS8, (last - first) * nrt * ROWS8)
+        extinct_all = flat[span, :]
+        flat[span, :] = heating_rate * extinct_all * jnp.exp(-(running_sums(extinct_all) - 0.5 * extinct_all))
+
+        @pl.loop(first, last)
         def _(cp):
             for q in range(nrt):
                 w = five(wet, cp, q)
@@ -400,10 +411,10 @@
         result[pl.ds(start, ROWS8, stride=nrt * ntr * inner), :] = value
 
     edge = halo // 2
-    ocean_step(ocean_a, ocean_b, stock_a)
+    ocean_step(ocean_a, ocean_b, stock_a, 0, ncp)
     substep(stock_a, stock_b, 0, ncp, finish_in(stock_b))
     substep(stock_b, stock_a, edge // 2, ncp - edge // 2, finish_in(stock_a))
-    ocean_step(ocean_b, ocean_a, stock_a)
+    ocean_step(ocean_b, ocean_a, stock_a, edge // 2, ncp - edge // 2)
     substep(stock_a, stock_b, edge // 2, ncp - edge // 2, finish_in(stock_b))
     substep(stock_b, stock_a, edge, ncp - edge, finish_out)
     send = pltpu.make_async_copy(result.at[pl.ds(halo * ntr * inner, rows * ntr * inner)], out, sem.at[0])
@@ -477,18 +488,7 @@
     margin = edge * LANES
     from_west = shift(ocean_fields[:, :, -margin:], "gx", 1)
     from_east = shift(ocean_fields[:, :, :margin], "gx", -1)
-    depth = wet_levels.astype(F32).reshape(tiles, columns // tiles)
-    blank = jnp.zeros((1, HALO), F32)
-    depth = jnp.concatenate(
-        [
-            jnp.concatenate([blank, depth[:-1, -HALO:]], axis=0),
-            depth,
-            jnp.concatenate([depth[1:, :HALO], blank], axis=0),
-            jnp.zeros((tiles, GROUP * LANES - columns // tiles - 2 * HALO), F32),
-        ],
-        axis=1,
-    )
-    sent = cut_windows(tracers.reshape(ntr, lines, 1, LANES), depth.reshape(tiles, GROUP, 1, LANES), tiles, ncp)
+    sent = cut_windows(tracers.reshape(ntr, lines, 1, LANES), wet_levels, tiles, ncp)
     tile = lax.all_to_all(sent.reshape(tiles, -1, LANES), "gx", split_axis=0, concat_axis=0, tiled=True)
     tile = tile.reshape(-1, LANES)
     to_north, to_south = row_messages(tile, from_west, ocean_fields, from_east, ncp)

time: 148 us -> 147 us (level)
  no operation moved by 1% of the time
where the time goes in v6:
time: 147 us
  waiting for transfers between devices  51.2 us (35%)
  blocking collectives  34.4 us (23%)
  Pallas kernels  33.6 us (23%)
  starting transfers between devices  24.8 us (17%)
  local copies, waits for them, and re-layouts  1.75 us (1%)
    ppermute x2, waiting for transfers between devices, shift(): return lax.ppermute(array, axis, [(i + 1, i) for i in range(count - 1)])  45.4 us
    all_to_all x1, blocking collectives, shards(): lax.all_to_all(result.reshape(tiles, ntr * inner, LANES), 'gx', split_axi...  34.4 us
    pallas_call x1, Pallas kernels, run_window(): pl.pallas_call(main_kernel, out_shape=(jax.ShapeDtypeStruct((4, rows, inn...  27.9 us
    all_to_all x1, starting transfers between devices, shards(): lax.all_to_all(sent.reshape(tiles, -1, LANES), 'gx', split_axis=0, concat...  11.6 us
    ppermute x2, starting transfers between devices, shift(): return lax.ppermute(array, axis, [(i, i + 1) for i in range(count - 1)])  10 us
    ppermute x2, waiting for transfers between devices, shift(): return lax.ppermute(array, axis, [(i, i + 1) for i in range(count - 1)])  4.7 us
    pallas_call x1, Pallas kernels, cut_windows(): pl.pallas_call(window_kernel, out_shape=jax.ShapeDtypeStruct((tiles, grou...  4.53 us
    ppermute x2, starting transfers between devices, shift(): return lax.ppermute(array, axis, [(i + 1, i) for i in range(count - 1)])  3.21 us
  transfers between devices with their start and end apart: 5, of which 4 were waited for; matrix products, arithmetic and copies ran while one was open for 0% of the time, Pallas kernels for 0%

profile of v6, /device:TPU:1, one launch (start us, length us, event | category | flops | bytes accessed | tf_op | source)
XLA Modules:
  0.0 146.5 jit_solution(15905525102133170509)
XLA Ops:
  0.6 4.5 %cut_windows.1 = f32[32,58,4,1,128]{4,3,2,1,0:T(1,128)} custom-call(f32[19,256,1,128]{3,2,1,0:T(1,128)} %bitcast.12, s32[1,512]{1,0:T(1,128)} %wet_levels.1), custom_call_target="tpu_custom_call" | custom-call | tf_op jit(solution)/shard_map/cut_windows/pallas_call | solution.py:99
  5.2 0.0 copy-start
  5.2 11.6 %all-to-all-start = ((f32[32,232,128]{2,1,0:T(8,128)}), f32[32,232,128]{2,1,0:T(8,128)}, u32[]{:S(2)}, u32[]{:S(2)}) async-start(f32[32,232,128]{2,1,0:T(8,128)} %bitcast.9), calls=%async_computation | async-start | bytes 7602176 | tf_op jit(solution)/shard_map/all_to_all | solution.py:492
  16.8 0.0 copy-done
  16.8 0.0 copy-start.1
  16.8 1.3 collective-permute-start.1
  18.1 4.0 %collective-permute-start = (f32[4,32,256]{2,1,0:T(8,128)S(1)}, f32[4,32,256]{2,1,0:T(8,128)S(1)}, u32[]{:S(2)}, u32[]{:S(2)}) collective-permute-start(f32[4,32,256]{2,1,0:T(8,128)S(1)} %get-tuple-element.11), channel_id=1, source_target_pairs={{0,1},{1,2},{2,3},{3,4},{4,5},{5,6},{6,7},{7,8},{8,9},{9,10},{10,1... | collective-permute-start | bytes 393224 | tf_op jit(solution)/shard_map/ppermute | solution.py:472
  22.1 41.0 %collective-permute-done.1.east = f32[4,32,256]{2,1,0:T(8,128)S(1)} collective-permute-done((f32[4,32,256]{2,1,0:T(8,128)S(1)}, f32[4,32,256]{2,1,0:T(8,128)S(1)}, u32[]{:S(2)}, u32[]{:S(2)}) %collective-permute-start.1) | collective-permute-done | bytes 131104 | tf_op jit(solution)/shard_map/ppermute | solution.py:473
  63.2 0.0 collective-permute-done.west
  63.2 1.0 all-to-all-done
  64.2 1.2 row_messages.1
  65.4 6.0 %collective-permute-start.2 = (f32[1120,128]{1,0:T(8,128)S(1)}, f32[1120,128]{1,0:T(8,128)S(1)}, u32[]{:S(2)}, u32[]{:S(2)}) collective-permute-start(f32[1120,128]{1,0:T(8,128)S(1)} %get-tuple-element.6), channel_id=1, source_target_pairs={{0,32},{32,64},{64,96},{1,33},{33,65},{65,97},{2,34},{34,66},{66,9... | collective-permute-start | bytes 1720328 | tf_op jit(solution)/shard_map/ppermute | solution.py:472
  71.5 1.9 %collective-permute-start.3 = (f32[1120,128]{1,0:T(8,128)S(1)}, f32[1120,128]{1,0:T(8,128)S(1)}, u32[]{:S(2)}, u32[]{:S(2)}) collective-permute-start(f32[1120,128]{1,0:T(8,128)S(1)} %get-tuple-element.7), channel_id=1, source_target_pairs={{32,0},{64,32},{96,64},{33,1},{65,33},{97,65},{34,2},{66,34},{98,6... | collective-permute-start | bytes 1720328 | tf_op jit(solution)/shard_map/ppermute | solution.py:473
  73.4 4.7 %collective-permute-done.2.south = f32[1120,128]{1,0:T(8,128)S(1)} collective-permute-done((f32[1120,128]{1,0:T(8,128)S(1)}, f32[1120,128]{1,0:T(8,128)S(1)}, u32[]{:S(2)}, u32[]{:S(2)}) %collective-permute-start.2) | collective-permute-done | bytes 573472 | tf_op jit(solution)/shard_map/ppermute | solution.py:472
  78.1 4.4 %collective-permute-done.3.north = f32[1120,128]{1,0:T(8,128)S(1)} collective-permute-done((f32[1120,128]{1,0:T(8,128)S(1)}, f32[1120,128]{1,0:T(8,128)S(1)}, u32[]{:S(2)}, u32[]{:S(2)}) %collective-permute-start.3) | collective-permute-done | bytes 573472 | tf_op jit(solution)/shard_map/ppermute | solution.py:473
  82.5 0.0 copy-done.1
  82.5 27.9 %window.1 = (f32[4,32,1024]{2,1,0:T(8,128)}, f32[4864,128]{1,0:T(8,128)S(1)}) custom-call(f32[7424,128]{1,0:T(8,128)} %bitcast.2.tile, f32[1120,128]{1,0:T(8,128)S(1)} %collective-permute-done.2.south, f32[1120,128]{1,0:T(8,128)S(1)} %collective-permute-done.3.north, f32[4,32,256]{2,1,0:T(8,128)S(1)} %collective-permute-done.west, ...), custom_call_target="tpu_custom_call" | custom-call | tf_op jit(solution)/shard_map/window/pallas_call | solution.py:437
  110.4 34.4 %all_to_all.10 = f32[32,152,128]{2,1,0:T(8,128)S(1)} all-to-all(f32[32,152,128]{2,1,0:T(8,128)S(1)} %bitcast.8), channel_id=1, replica_groups=mesh['grp'=4,'gx'=32] {'gx'}, dimensions={0} | all-to-all | bytes 4980736 | tf_op jit(solution)/shard_map/all_to_all | solution.py:500
  144.8 1.7 %copy.6 = f32[32,19,8,128]{3,2,0,1:T(8,128)} copy(f32[32,19,8,128]{3,2,1,0:T(8,128)S(1)} %bitcast.10) | data formatting | bytes 4980736 | tf_op jit(solution)/shard_map/reshape | solution.py:501
  (1 shorter events, 0.0 us)
Async XLA Ops:
  5.2 11.6 %copy-start = (f32[4,32,1024]{2,1,0:T(8,128)S(1)}, f32[4,32,1024]{2,1,0:T(8,128)}, u32[]{:S(2)}) copy-start(f32[4,32,1024]{2,1,0:T(8,128)} %ocean.3) | copy-start | bytes 1572868
  5.2 59.0 %all-to-all-start = ((f32[32,232,128]{2,1,0:T(8,128)}), f32[32,232,128]{2,1,0:T(8,128)}, u32[]{:S(2)}, u32[]{:S(2)}) async-start(f32[32,232,128]{2,1,0:T(8,128)} %bitcast.9), calls=%async_computation | async-start | bytes 7602176 | tf_op jit(solution)/shard_map/all_to_all | solution.py:492
  16.8 65.7 %copy-start.1 = (f32[19,19]{1,0:T(8,128)S(1)}, f32[19,19]{1,0:T(8,128)}, u32[]{:S(2)}) copy-start(f32[19,19]{1,0:T(8,128)} %mix_ref.1) | copy-start | bytes 4336
  16.8 46.3 %collective-permute-start.1 = (f32[4,32,256]{2,1,0:T(8,128)S(1)}, f32[4,32,256]{2,1,0:T(8,128)S(1)}, u32[]{:S(2)}, u32[]{:S(2)}) collective-permute-start(f32[4,32,256]{2,1,0:T(8,128)S(1)} %get-tuple-element.10), channel_id=1, source_target_pairs={{1,0},{2,1},{3,2},{4,3},{5,4},{6,5},{7,6},{8,7},{9,8},{10,9},{11,1... | collective-permute-start | bytes 393224 | tf_op jit(solution)/shard_map/ppermute | solution.py:473
  18.1 45.0 %collective-permute-start = (f32[4,32,256]{2,1,0:T(8,128)S(1)}, f32[4,32,256]{2,1,0:T(8,128)S(1)}, u32[]{:S(2)}, u32[]{:S(2)}) collective-permute-start(f32[4,32,256]{2,1,0:T(8,128)S(1)} %get-tuple-element.11), channel_id=1, source_target_pairs={{0,1},{1,2},{2,3},{3,4},{4,5},{5,6},{6,7},{7,8},{8,9},{9,10},{10,1... | collective-permute-start | bytes 393224 | tf_op jit(solution)/shard_map/ppermute | solution.py:472
  65.4 12.7 %collective-permute-start.2 = (f32[1120,128]{1,0:T(8,128)S(1)}, f32[1120,128]{1,0:T(8,128)S(1)}, u32[]{:S(2)}, u32[]{:S(2)}) collective-permute-start(f32[1120,128]{1,0:T(8,128)S(1)} %get-tuple-element.6), channel_id=1, source_target_pairs={{0,32},{32,64},{64,96},{1,33},{33,65},{65,97},{2,34},{34,66},{66,9... | collective-permute-start | bytes 1720328 | tf_op jit(solution)/shard_map/ppermute | solution.py:472
  71.5 11.0 %collective-permute-start.3 = (f32[1120,128]{1,0:T(8,128)S(1)}, f32[1120,128]{1,0:T(8,128)S(1)}, u32[]{:S(2)}, u32[]{:S(2)}) collective-permute-start(f32[1120,128]{1,0:T(8,128)S(1)} %get-tuple-element.7), channel_id=1, source_target_pairs={{32,0},{64,32},{96,64},{33,1},{65,33},{97,65},{34,2},{66,34},{98,6... | collective-permute-start | bytes 1720328 | tf_op jit(solution)/shard_map/ppermute | solution.py:473
